TPU v7x, 256 devices: a whole 4x4x8 slice. The times are simulated.
256 devices in a mesh: dp: 4 (over y_lo, core), context: 64 (over y_hi, z, x).
Axes of the slice: x: 4, y: 4 (y_hi: 2, y_lo: 2; y = y_hi * 2 + y_lo), z: 8, core: 2. Of those that a mesh axis runs over, the one named last changes fastest.
Arguments:
- queries: bfloat16 [4, 1024, 8192], P('dp', None, 'context'), may hold values from -6 to 6
- key_stream: bfloat16 [4, 1024, 8192], P('dp', None, 'context'), may hold values from -6 to 6
- value_stream: bfloat16 [4, 1024, 8192], P('dp', None, 'context'), may hold values from -6 to 6
- cotangent: bfloat16 [4, 1024, 8192], P('dp', None, 'context'), may hold values from -6 to 6
- short_taps: float32 [3, 3, 1024], replicated, may hold values from -2 to 2
- residues: float32 [1024, 16], P('context'), may hold values from -1.5 to 1.5
- decay_rates: float32 [1024, 16], P('context'), as said below
Outputs:
- output: bfloat16 [4, 1024, 8192], P('dp', None, 'context')
- adjoint_queries: bfloat16 [4, 1024, 8192], P('dp', None, 'context')
- adjoint_keys: bfloat16 [4, 1024, 8192], P('dp', None, 'context')
- adjoint_values: bfloat16 [4, 1024, 8192], P('dp', None, 'context')
- adjoint_taps: float32 [3, 3, 1024], replicated
- adjoint_residues: float32 [1024, 16], P('context')
- adjoint_decays: float32 [1024, 16], P('context')
Inputs may be any that keep to these rules, and one draw needn't show every extreme that they name: `decay_rates`: every rate lies between 1 / 16384 and 0.05.
All inputs are finite; a program needn't handle non-finite values.
Results may differ from a plain program's by a relative error of at most 0.017.
Values may be sent and summed in bfloat16 or wider, within the bound.
A program may use at most 128 MiB of HBM per device.

v0:
```python
import math

import jax
import jax.numpy as jnp
from jax import lax
from jax.sharding import PartitionSpec as P

HIGHEST_PRECISION = lax.Precision.HIGHEST


def passed_along(x, axis, by):
    peers = lax.axis_size(axis)
    pairs = [(i, i + by) for i in range(peers) if 0 <= i + by < peers]
    return lax.ppermute(x, axis, pairs)


def dft_tables(seq_length):
    total_len = 2 * seq_length
    col_count = min(256, seq_length)
    row_count = total_len // col_count
    half_rows = row_count // 2
    row_index = jnp.arange(row_count, dtype=jnp.int32)
    half_index = jnp.arange(half_rows, dtype=jnp.int32)
    col_index = jnp.arange(col_count, dtype=jnp.int32)
    first_angle = (row_index[:, None] * half_index[None, :] % row_count).astype(jnp.float32) * (
        2.0 * math.pi / row_count
    )
    twist_angle = (row_index[:, None] * col_index[None, :] % total_len).astype(jnp.float32) * (
        2.0 * math.pi / total_len
    )
    second_angle = (col_index[:, None] * col_index[None, :] % col_count).astype(jnp.float32) * (
        2.0 * math.pi / col_count
    )
    return (
        jnp.cos(first_angle),
        jnp.sin(first_angle),
        jnp.cos(twist_angle),
        jnp.sin(twist_angle),
        jnp.cos(second_angle),
        jnp.sin(second_angle),
    )


def along_cols(array, table):
    return jnp.einsum("bckm,mj->bckj", array, table, precision=HIGHEST_PRECISION)


def forward_dft(signal, tables):
    cos_first, sin_first, cos_twist, sin_twist, cos_second, sin_second = tables
    batch_here, chan_here, seq_length = signal.shape
    folded = signal.reshape(batch_here, chan_here, cos_first.shape[1], cos_second.shape[0])
    part_re = jnp.einsum("kn,bcnm->bckm", cos_first, folded, precision=HIGHEST_PRECISION)
    part_im = -jnp.einsum("kn,bcnm->bckm", sin_first, folded, precision=HIGHEST_PRECISION)
    twist_re = part_re * cos_twist + part_im * sin_twist
    twist_im = part_im * cos_twist - part_re * sin_twist
    spec_re = along_cols(twist_re, cos_second) + along_cols(twist_im, sin_second)
    spec_im = along_cols(twist_im, cos_second) - along_cols(twist_re, sin_second)
    return (spec_re, spec_im)


def inverse_dft(spec_re, spec_im, tables):
    cos_first, sin_first, cos_twist, sin_twist, cos_second, sin_second = tables
    back_re = along_cols(spec_re, cos_second) - along_cols(spec_im, sin_second)
    back_im = along_cols(spec_im, cos_second) + along_cols(spec_re, sin_second)
    turn_re = back_re * cos_twist - back_im * sin_twist
    turn_im = back_im * cos_twist + back_re * sin_twist
    folded = jnp.einsum(
        "kn,bckm->bcnm", cos_first, turn_re, precision=HIGHEST_PRECISION
    ) - jnp.einsum("kn,bckm->bcnm", sin_first, turn_im, precision=HIGHEST_PRECISION)
    batch_here, chan_here, half_rows, col_count = folded.shape
    return folded.reshape(batch_here, chan_here, half_rows * col_count) / (
        2.0 * half_rows * col_count
    )


def freq_grid(seq_length, tables):
    row_count = tables[2].shape[0]
    col_count = tables[2].shape[1]
    total_len = 2 * seq_length
    freq_index = (
        jnp.arange(row_count, dtype=jnp.int32)[:, None]
        + row_count * jnp.arange(col_count, dtype=jnp.int32)[None, :]
    )
    signed_index = jnp.where(freq_index >= seq_length, freq_index - total_len, freq_index)
    angle = signed_index.astype(jnp.float32) * (2.0 * math.pi / total_len)
    half_sine = jnp.sin(0.5 * angle)
    return (half_sine * half_sine, jnp.sin(angle), freq_index % 2 == 0)


def mode_response(decay, half_square, sine, is_even, seq_length):
    damping = jnp.exp(-decay)
    amplitude = jnp.sqrt(-jnp.expm1(-2.0 * decay))
    numerator = jnp.where(
        is_even, -jnp.expm1(-decay * seq_length), 1.0 + jnp.exp(-decay * seq_length)
    )
    real_den = -jnp.expm1(-decay) + 2.0 * damping * half_square
    imag_den = damping * sine
    factor = amplitude * numerator / (real_den * real_den + imag_den * imag_den)
    return (factor * real_den, -factor * imag_den)


def filter_spectrum(residues, decay_rates, grid, seq_length):
    half_square, sine, is_even = grid

    def add_mode(carry, inputs):
        residue_col, decay_col = inputs
        resp_re, resp_im = mode_response(
            decay_col[:, None, None], half_square, sine, is_even, seq_length
        )
        weight_col = residue_col[:, None, None]
        return ((carry[0] + weight_col * resp_re, carry[1] + weight_col * resp_im), None)

    empty = jnp.zeros((residues.shape[0],) + sine.shape, jnp.float32)
    spectra, unused = lax.scan(add_mode, (empty, empty), (residues.T, decay_rates.T))
    return spectra


def mode_adjoints(residues, decay_rates, adj_re, adj_im, grid, seq_length):
    half_square, sine, is_even = grid

    def one_mode(carry, inputs):
        residue_col, decay_col = inputs
        decay_cube = decay_col[:, None, None]

        def response(decay_value):
            return mode_response(decay_value, half_square, sine, is_even, seq_length)

        values, tangents = jax.jvp(response, (decay_cube,), (jnp.ones_like(decay_cube),))
        residue_term = jnp.sum(adj_re * values[0] + adj_im * values[1], axis=(1, 2))
        decay_term = (
            jnp.sum(adj_re * tangents[0] + adj_im * tangents[1], axis=(1, 2))
            * residue_col
            * decay_col
        )
        return (carry, (residue_term, decay_term))

    unused, terms = lax.scan(one_mode, jnp.zeros((), jnp.float32), (residues.T, decay_rates.T))
    return (terms[0].T, terms[1].T)


def owner_work(gated, upstream, residues, decay_rates):
    seq_length = gated.shape[2]
    tables = dft_tables(seq_length)
    grid = freq_grid(seq_length, tables)
    spec_re, spec_im = filter_spectrum(residues, decay_rates, grid, seq_length)

    def convolve(signal, filt_re, filt_im):
        sig_re, sig_im = forward_dft(signal, tables)
        return inverse_dft(
            sig_re * filt_re - sig_im * filt_im, sig_re * filt_im + sig_im * filt_re, tables
        )

    mixed_exact, pullback = jax.vjp(convolve, gated.astype(jnp.float32), spec_re, spec_im)
    source_adj, adj_re, adj_im = pullback(upstream.astype(jnp.float32))
    residue_adj, decay_adj = mode_adjoints(residues, decay_rates, adj_re, adj_im, grid, seq_length)
    return (
        mixed_exact.astype(jnp.bfloat16),
        source_adj.astype(jnp.bfloat16),
        residue_adj,
        decay_adj,
    )


def featurize(extended, weights, length_here):
    reach_back = weights.shape[0] - 1
    result = jnp.zeros(extended[:, :, :length_here].shape, jnp.float32)
    for offset in range(reach_back + 1):
        start_at = reach_back - offset
        result = (
            result
            + weights[offset][None, :, None] * extended[:, :, start_at : start_at + length_here]
        )
    return result


def per_device(queries, key_stream, value_stream, cotangent, short_taps, residues, decay_rates):
    reach_back = short_taps.shape[1] - 1
    length_here = queries.shape[2]
    rim_parts = passed_along(
        (
            queries[:, :, length_here - reach_back :],
            key_stream[:, :, length_here - reach_back :],
            value_stream[:, :, length_here - reach_back :],
        ),
        "context",
        1,
    )
    extended = [
        jnp.concatenate([rim_part, signal], axis=2).astype(jnp.float32)
        for signal, rim_part in zip((queries, key_stream, value_stream), rim_parts)
    ]
    query_short, key_short, value_short = [
        featurize(extended[stream], short_taps[stream], length_here).astype(jnp.bfloat16)
        for stream in range(3)
    ]
    upstream = (cotangent.astype(jnp.float32) * query_short.astype(jnp.float32)).astype(
        jnp.bfloat16
    )
    key_own, value_own, upstream_own = (
        lax.all_to_all(key_short, "context", split_axis=1, concat_axis=2, tiled=True),
        lax.all_to_all(value_short, "context", split_axis=1, concat_axis=2, tiled=True),
        lax.all_to_all(upstream, "context", split_axis=1, concat_axis=2, tiled=True),
    )
    gated_own = (key_own.astype(jnp.float32) * value_own.astype(jnp.float32)).astype(jnp.bfloat16)
    mixed_own, source_own, residue_adj, decay_adj = owner_work(
        gated_own, upstream_own, residues, decay_rates
    )
    key_adj_own = (source_own.astype(jnp.float32) * value_own.astype(jnp.float32)).astype(
        jnp.bfloat16
    )
    value_adj_own = (source_own.astype(jnp.float32) * key_own.astype(jnp.float32)).astype(
        jnp.bfloat16
    )
    mixed_seq, key_adj, value_adj = (
        lax.all_to_all(mixed_own, "context", split_axis=2, concat_axis=1, tiled=True),
        lax.all_to_all(key_adj_own, "context", split_axis=2, concat_axis=1, tiled=True),
        lax.all_to_all(value_adj_own, "context", split_axis=2, concat_axis=1, tiled=True),
    )
    output = (query_short.astype(jnp.float32) * mixed_seq.astype(jnp.float32)).astype(jnp.bfloat16)
    query_adj = (cotangent.astype(jnp.float32) * mixed_seq.astype(jnp.float32)).astype(jnp.bfloat16)
    stream_adjs = (query_adj, key_adj, value_adj)
    next_parts = passed_along(
        (query_adj[:, :, :reach_back], key_adj[:, :, :reach_back], value_adj[:, :, :reach_back]),
        "context",
        -1,
    )
    signal_adjs = []
    tap_rows = []
    for stream in range(3):
        adjoint_f = stream_adjs[stream].astype(jnp.float32)
        ahead = jnp.concatenate([stream_adjs[stream], next_parts[stream]], axis=2).astype(
            jnp.float32
        )
        total_adj = jnp.zeros(adjoint_f.shape, jnp.float32)
        per_tap = []
        for offset in range(reach_back + 1):
            total_adj = (
                total_adj
                + short_taps[stream, offset][None, :, None]
                * ahead[:, :, offset : offset + length_here]
            )
            start_at = reach_back - offset
            per_tap.append(
                jnp.sum(
                    adjoint_f * extended[stream][:, :, start_at : start_at + length_here],
                    axis=(0, 2),
                )
            )
        signal_adjs.append(total_adj.astype(jnp.bfloat16))
        tap_rows.append(jnp.stack(per_tap))
    tap_part = jnp.stack(tap_rows)
    token_scale = 1.0 / math.sqrt(
        queries.shape[0] * lax.axis_size("dp") * length_here * lax.axis_size("context")
    )
    tap_total = lax.psum(tap_part, ("dp", "context"))
    residue_own, decay_own = lax.psum((residue_adj, decay_adj), "dp")
    return (
        output,
        signal_adjs[0],
        signal_adjs[1],
        signal_adjs[2],
        tap_total * token_scale,
        residue_own * token_scale,
        decay_own * token_scale,
    )


def solution(mesh):
    in_specs = (
        P("dp", None, "context"),
        P("dp", None, "context"),
        P("dp", None, "context"),
        P("dp", None, "context"),
        P(),
        P("context", None),
        P("context", None),
    )
    out_specs = (
        P("dp", None, "context"),
        P("dp", None, "context"),
        P("dp", None, "context"),
        P("dp", None, "context"),
        P(),
        P("context", None),
        P("context", None),
    )
    return jax.shard_map(
        per_device, mesh=mesh, in_specs=in_specs, out_specs=out_specs, check_vma=False
    )
```

profile of v0, /device:TPU:230, one launch (start us, length us, event | category | flops | bytes accessed | tf_op | source)
XLA Modules:
  0.0 640.2 jit_solution(5047321556675018098)
XLA Ops:
  4.7 7.0 %collective-permute-done.1 = bf16[1,1024,2]{2,1,0:T(8,128)(2,1)S(1)} collective-permute-done((bf16[1,1024,2]{2,1,0:T(8,128)(2,1)S(1)}, bf16[1,1024,2]{2,1,0:T(8,128)(2,1)S(1)}, u32[]{:S(2)}, u32[]{:S(2)}) %collective-permute-start.1) | collective-permute-done | bytes 4128 | tf_op jit(solution)/shard_map/ppermute | solution.py:14
  15.7 2.2 reduce
  18.7 12.4 %all-to-all-start = ((bf16[64,2,1024]{2,1,0:T(2,128)(2,1)}), bf16[64,2,1024]{2,1,0:T(2,128)(2,1)S(1)}, u32[]{:S(2)}, u32[]{:S(2)}) async-start(bf16[64,2,1024]{2,1,0:T(2,128)(2,1)} %reshape.877), calls=%async_computation | async-start | bytes 524288 | tf_op jit(solution)/shard_map/all_to_all | solution.py:200
  31.3 4.9 collective-permute-start.2
  37.1 3.4 collective-permute-start
  44.2 2.3 reduce.1
  47.2 13.0 %all-to-all-start.1 = ((bf16[64,2,1024]{2,1,0:T(2,128)(2,1)}), bf16[64,2,1024]{2,1,0:T(2,128)(2,1)S(1)}, u32[]{:S(2)}, u32[]{:S(2)}) async-start(bf16[64,2,1024]{2,1,0:T(2,128)(2,1)} %reshape.879), calls=%async_computation.1 | async-start | bytes 524288 | tf_op jit(solution)/shard_map/all_to_all | solution.py:201
  60.3 47.8 %while.33 = (s32[]{:T(128)}, f32[16,64,256]{2,1,0:T(8,128)S(1)}, f32[16,64,256]{2,1,0:T(8,128)S(1)}, f32[16,16]{1,0:T(8,128)}, f32[16,16]{1,0:T(8,128)}, /*index=5*/s32[256]{0:T(256)S(1)}, s32[]{:T(128)}, s32[]{:T(128)}) while((s32[]{:T(128)}, f32[16,64,256]{2,1,0:T(8,128)S(1)}, ...), condition=%wide.region_1.2_spmd.clone.clone.clone, body=%wide.region_0.1_spmd.clone.clone.clone.sunk | while | flops 5062803 | bytes 4492583 | solution.py:114
  113.7 2.3 reduce.2
  116.8 13.0 %all-to-all-start.3 = ((bf16[64,2,1024]{2,1,0:T(2,128)(2,1)}), bf16[64,2,1024]{2,1,0:T(2,128)(2,1)}, u32[]{:S(2)}, u32[]{:S(2)}) async-start(bf16[64,2,1024]{2,1,0:T(2,128)(2,1)} %reshape.883), calls=%async_computation.3 | async-start | bytes 524288 | tf_op jit(solution)/shard_map/all_to_all | solution.py:202
  134.9 4.8 all-to-all-done.3
  139.7 3.1 reshape.884
  147.3 2.1 convolution_bitcast_fusion
  149.5 2.2 convolution_bitcast_fusion.1
  159.8 2.2 convolution_add_fusion.5
  166.0 3.9 multiply_add_fusion.3
  169.9 3.0 fusion.132
  172.9 3.2 fusion.77
  187.7 6.7 %copy.214 = bf16[1,16,8192]{1,0,2:T(2,128)(2,1)} copy(bf16[1,16,8192]{2,1,0:T(8,128)(2,1)S(1)} %convert_element_type.446) | data formatting | bytes 524288 | tf_op jit(solution)/shard_map/convert_element_type | solution.py:157
  194.4 47.1 %reduce.3 = bf16[8192,16]{1,0:T(8,128)(2,1)} reduce(bf16[8192,1,16]{2,1,0:T(2,128)(2,1)} %bitcast.310, bf16[]{:T(256)} %broadcast.596), dimensions={1}, to_apply=%bitcast.253.reduce_sub_computation | reduce | bytes 524290
  241.5 4.4 reshape.881
  245.9 8.5 %all-to-all-start.2 = ((bf16[64,2,1024]{2,1,0:T(2,128)(2,1)}), bf16[64,2,1024]{2,1,0:T(2,128)(2,1)S(1)}, u32[]{:S(2)}, u32[]{:S(2)}) async-start(bf16[64,2,1024]{2,1,0:T(2,128)(2,1)} %reshape.881), calls=%async_computation.2 | async-start | bytes 524288 | tf_op jit(solution)/shard_map/all_to_all | solution.py:215
  254.4 3.2 convolution_add_fusion.1
  257.6 3.2 convolution_add_fusion
  262.7 2.7 copy.231
  265.3 2.6 copy.221
  267.9 2.6 copy.225
  270.6 9.7 %multiply_convert_fusion = (bf16[1,16,8192]{1,0,2:T(2,128)(2,1)}, bf16[1,16,8192]{1,0,2:T(2,128)(2,1)}) fusion(f32[1,16,8192]{1,0,2:T(1,128)} %bitcast.306, f32[1,16,8192]{1,0,2:T(1,128)} %bitcast.308, f32[1,16,8192]{1,0,2:T(1,128)} %bitcast.307), kind=kLoop, calls=%fused_computation.90 | loop fusion | flops 524288 | bytes 2097152 | tf_op jit(solution)/shard_map/convert_element_type | solution.py:211
  280.3 46.9 %reduce.4 = bf16[8192,16]{1,0:T(8,128)(2,1)} reduce(bf16[8192,1,16]{2,1,0:T(2,128)(2,1)} %bitcast.309, bf16[]{:T(256)} %broadcast.596), dimensions={1}, to_apply=%bitcast.257.reduce_sub_computation | reduce | bytes 524290
  327.2 4.4 reshape.885
  331.6 13.4 %all-to-all-start.4 = ((bf16[64,2,1024]{2,1,0:T(2,128)(2,1)}), bf16[64,2,1024]{2,1,0:T(2,128)(2,1)}, u32[]{:S(2)}, u32[]{:S(2)}) async-start(bf16[64,2,1024]{2,1,0:T(2,128)(2,1)} %reshape.885), calls=%async_computation.4 | async-start | bytes 524288 | tf_op jit(solution)/shard_map/all_to_all | solution.py:216
  345.1 67.6 %while.32 = (s32[]{:T(128)}, f32[16,16]{1,0:T(8,128)S(1)}, f32[16,16]{1,0:T(8,128)S(1)}, f32[16,16]{1,0:T(8,128)}, f32[16,64,256]{2,1,0:T(8,128)S(1)}, /*index=5...) while((s32[]{:T(128)}, f32[16,16]{1,0:T(8,128)S(1)}, ...), condition=%wide.region_15.16_spmd.clone.clone.clone, body=%wide.region_12.15_spmd.clone.clone.clone.sunk | while | flops 12403026 | bytes 2396661 | solution.py:137
  346.3 2.2 fusion.310
  350.6 2.2 fusion.310
  354.8 2.2 fusion.310
  359.0 2.2 fusion.310
  363.2 2.2 fusion.310
  367.5 2.2 fusion.310
  371.7 2.2 fusion.310
  375.9 2.2 fusion.310
  380.1 2.2 fusion.310
  384.4 2.2 fusion.310
  388.6 2.2 fusion.310
  392.8 2.2 fusion.310
  397.0 2.2 fusion.310
  401.3 2.2 fusion.310
  405.5 2.2 fusion.310
  409.7 2.2 fusion.310
  412.8 45.3 %reduce.5 = bf16[8192,16]{1,0:T(8,128)(2,1)S(1)} reduce(bf16[8192,1,16]{2,1,0:T(2,128)(2,1)} %bitcast.305, bf16[]{:T(256)} %broadcast.596), dimensions={1}, to_apply=%bitcast.259.reduce_sub_computation | reduce | bytes 524290
  458.1 2.9 reshape.887
  461.0 10.4 %all-reduce = (f32[16,16]{1,0:T(8,128)S(1)}, f32[16,16]{1,0:T(8,128)S(1)}) all-reduce(f32[16,16]{1,0:T(8,128)S(1)} %bitcast.355, f32[16,16]{1,0:T(8,128)S(1)} %bitcast.356), channel_id=1, replica_groups=mesh['dp'=4,'context'=64] {'dp'}, use_global_device_ids=true, to_apply=%region_16.17 | all-reduce | flops 512 | bytes 4096 | tf_op jit(solution)/shard_map/psum | solution.py:256
  472.6 7.6 %reshape.882 = bf16[8192,1,16]{2,1,0:T(2,128)(2,1)} reshape(bf16[64,2,1024]{2,1,0:T(2,128)(2,1)S(1)} %all-to-all-done.2) | data formatting | bytes 524288
  480.2 7.9 %copy.215 = bf16[1,16,8192]{2,1,0:T(8,128)(2,1)S(1)} copy(bf16[1,16,8192]{1,0,2:T(2,128)(2,1)} %bitcast.311) | data formatting | bytes 524288 | tf_op jit(solution)/shard_map/all_to_all | solution.py:215
  488.1 13.0 %all-to-all-start.5 = ((bf16[64,2,1024]{2,1,0:T(2,128)(2,1)}), bf16[64,2,1024]{2,1,0:T(2,128)(2,1)S(1)}, u32[]{:S(2)}, u32[]{:S(2)}) async-start(bf16[64,2,1024]{2,1,0:T(2,128)(2,1)} %reshape.887), calls=%async_computation.5 | async-start | bytes 524288 | tf_op jit(solution)/shard_map/all_to_all | solution.py:217
  501.6 9.9 %reshape.886 = bf16[8192,1,16]{2,1,0:T(2,128)(2,1)} reshape(bf16[64,2,1024]{2,1,0:T(2,128)(2,1)} %all-to-all-done.4) | data formatting | bytes 524288
  511.4 7.9 %copy.223 = bf16[1,16,8192]{2,1,0:T(8,128)(2,1)S(1)} copy(bf16[1,16,8192]{1,0,2:T(2,128)(2,1)} %bitcast.312) | data formatting | bytes 524288 | tf_op jit(solution)/shard_map/all_to_all | solution.py:216
  520.3 7.6 %reshape.888 = bf16[8192,1,16]{2,1,0:T(2,128)(2,1)} reshape(bf16[64,2,1024]{2,1,0:T(2,128)(2,1)S(1)} %all-to-all-done.5) | data formatting | bytes 524288
  528.0 8.0 %copy.227 = bf16[1,16,8192]{2,1,0:T(8,128)(2,1)S(1)} copy(bf16[1,16,8192]{1,0,2:T(2,128)(2,1)} %bitcast.313) | data formatting | bytes 524288 | tf_op jit(solution)/shard_map/all_to_all | solution.py:217
  537.1 2.5 fusion.91
  539.6 75.4 %psum.21 = f32[3,3,1024]{2,1,0:T(4,128)S(1)} all-reduce(f32[3,3,1024]{2,1,0:T(4,128)S(1)} %pad_maximum_fusion), channel_id=1, replica_groups=mesh['dp'=4,'context'=64] {'dp','context'}, use_global_device_ids=true, to_apply=%region_11.12 | all-reduce | flops 9216 | bytes 73728 | tf_op jit(solution)/shard_map/psum | solution.py:255
  617.6 3.3 collective-permute-start.4
  621.1 2.6 collective-permute-start.3
  623.7 8.1 %collective-permute-done.5 = bf16[1,1024,2]{2,1,0:T(8,128)(2,1)S(1)} collective-permute-done((bf16[1,1024,2]{2,1,0:T(8,128)(2,1)S(1)}, bf16[1,1024,2]{2,1,0:T(8,128)(2,1)S(1)}, u32[]{:S(2)}, u32[]{:S(2)}) %collective-permute-start.5) | collective-permute-done | bytes 4128 | tf_op jit(solution)/shard_map/ppermute | solution.py:14
  633.4 3.0 collective-permute-done.4
  (390 shorter events, 145.6 us)
Async XLA Ops:
  0.6 30.5 %copy-start.19 = (bf16[1,1024,128]{2,1,0:T(8,128)(2,1)S(1)}, bf16[1,1024,128]{2,1,0:T(8,128)(2,1)}, u32[]{:S(2)}) copy-start(bf16[1,1024,128]{2,1,0:T(8,128)(2,1)} %param.13) | copy-start | bytes 786436
  0.6 35.5 %copy-start.20 = (bf16[1,1024,128]{2,1,0:T(8,128)(2,1)S(1)}, bf16[1,1024,128]{2,1,0:T(8,128)(2,1)}, u32[]{:S(2)}) copy-start(bf16[1,1024,128]{2,1,0:T(8,128)(2,1)} %param.11) | copy-start | bytes 786436
  0.7 39.8 %copy-start.33 = (f32[16,16]{1,0:T(8,128)S(1)}, f32[16,16]{1,0:T(8,128)}, u32[]{:S(2)}) copy-start(f32[16,16]{1,0:T(8,128)} %param.16) | copy-start | bytes 3076
  0.7 40.5 %copy-start.34 = (f32[16,16]{1,0:T(8,128)S(1)}, f32[16,16]{1,0:T(8,128)}, u32[]{:S(2)}) copy-start(f32[16,16]{1,0:T(8,128)} %param.17) | copy-start | bytes 3076
  1.8 9.9 %collective-permute-start.1 = (bf16[1,1024,2]{2,1,0:T(8,128)(2,1)S(1)}, bf16[1,1024,2]{2,1,0:T(8,128)(2,1)S(1)}, u32[]{:S(2)}, u32[]{:S(2)}) collective-permute-start(bf16[1,1024,2]{2,1,0:T(8,128)(2,1)S(1)} %slice.146), channel_id=1, source_target_pairs={{0,1},{1,2},{2,3},{3,4},{4,5},{5,6},{6,7},{7,8},{8,9},{9,10},{10,1... | collective-permute-start | bytes 12296 | tf_op jit(solution)/shard_map/ppermute | solution.py:14
  4.7 26.4 %copy-start.21 = (f32[1,1,1024]{2,1,0:T(1,128)}, f32[1,1,1024]{2,1,0:T(1,128)S(1)}, u32[]{:S(2)}) copy-start(f32[1,1,1024]{2,1,0:T(1,128)S(1)} %get-tuple-element.452) | copy-start | bytes 12292
  4.7 26.4 %copy-start.23 = (f32[1,1,1024]{2,1,0:T(1,128)}, f32[1,1,1024]{2,1,0:T(1,128)S(1)}, u32[]{:S(2)}) copy-start(f32[1,1,1024]{2,1,0:T(1,128)S(1)} %get-tuple-element.453) | copy-start | bytes 12292
  4.7 26.4 %copy-start.25 = (f32[1,1,1024]{2,1,0:T(1,128)}, f32[1,1,1024]{2,1,0:T(1,128)S(1)}, u32[]{:S(2)}) copy-start(f32[1,1,1024]{2,1,0:T(1,128)S(1)} %get-tuple-element.454) | copy-start | bytes 12292
  4.7 37.4 %copy-start.27 = (f32[1,1,1024]{2,1,0:T(1,128)}, f32[1,1,1024]{2,1,0:T(1,128)S(1)}, u32[]{:S(2)}) copy-start(f32[1,1,1024]{2,1,0:T(1,128)S(1)} %get-tuple-element.451) | copy-start | bytes 12292
  4.7 37.4 %copy-start.29 = (f32[1,1,1024]{2,1,0:T(1,128)}, f32[1,1,1024]{2,1,0:T(1,128)S(1)}, u32[]{:S(2)}) copy-start(f32[1,1,1024]{2,1,0:T(1,128)S(1)} %get-tuple-element.458) | copy-start | bytes 12292
  4.7 37.4 %copy-start.31 = (f32[1,1,1024]{2,1,0:T(1,128)}, f32[1,1,1024]{2,1,0:T(1,128)S(1)}, u32[]{:S(2)}) copy-start(f32[1,1,1024]{2,1,0:T(1,128)S(1)} %get-tuple-element.459) | copy-start | bytes 12292
  12.9 1.0 copy-start.4
  18.7 28.5 %all-to-all-start = ((bf16[64,2,1024]{2,1,0:T(2,128)(2,1)}), bf16[64,2,1024]{2,1,0:T(2,128)(2,1)S(1)}, u32[]{:S(2)}, u32[]{:S(2)}) async-start(bf16[64,2,1024]{2,1,0:T(2,128)(2,1)} %reshape.877), calls=%async_computation | async-start | bytes 524288 | tf_op jit(solution)/shard_map/all_to_all | solution.py:200
  31.3 10.5 %collective-permute-start.2 = (bf16[1,1024,2]{2,1,0:T(8,128)(2,1)S(1)}, bf16[1,1024,2]{2,1,0:T(8,128)(2,1)S(1)}, u32[]{:S(2)}, u32[]{:S(2)}) collective-permute-start(bf16[1,1024,2]{2,1,0:T(8,128)(2,1)S(1)} %slice.153), channel_id=1, source_target_pairs={{0,1},{1,2},{2,3},{3,4},{4,5},{5,6},{6,7},{7,8},{8,9},{9,10},{10,1... | collective-permute-start | bytes 12296 | tf_op jit(solution)/shard_map/ppermute | solution.py:14
  37.1 71.1 %collective-permute-start = (bf16[1,1024,2]{1,2,0:T(2,128)(2,1)}, bf16[1,1024,2]{1,2,0:T(2,128)(2,1)}, u32[]{:S(2)}, u32[]{:S(2)}) collective-permute-start(bf16[1,1024,2]{1,2,0:T(2,128)(2,1)} %copy.232), channel_id=1, source_target_pairs={{0,1},{1,2},{2,3},{3,4},{4,5},{5,6},{6,7},{7,8},{8,9},{9,10},{10,1... | collective-permute-start | bytes 12296 | tf_op jit(solution)/shard_map/ppermute | solution.py:14
  42.1 1.0 copy-start.6
  47.2 69.6 %all-to-all-start.1 = ((bf16[64,2,1024]{2,1,0:T(2,128)(2,1)}), bf16[64,2,1024]{2,1,0:T(2,128)(2,1)S(1)}, u32[]{:S(2)}, u32[]{:S(2)}) async-start(bf16[64,2,1024]{2,1,0:T(2,128)(2,1)} %reshape.879), calls=%async_computation.1 | async-start | bytes 524288 | tf_op jit(solution)/shard_map/all_to_all | solution.py:201
  60.3 51.6 %copy-start.17 = (bf16[1,1024,128]{2,1,0:T(8,128)(2,1)S(1)}, bf16[1,1024,128]{2,1,0:T(8,128)(2,1)}, u32[]{:S(2)}) copy-start(bf16[1,1024,128]{2,1,0:T(8,128)(2,1)} %param.14) | copy-start | bytes 786436
  110.9 1.0 copy-start.8
  116.8 22.9 %all-to-all-start.3 = ((bf16[64,2,1024]{2,1,0:T(2,128)(2,1)}), bf16[64,2,1024]{2,1,0:T(2,128)(2,1)}, u32[]{:S(2)}, u32[]{:S(2)}) async-start(bf16[64,2,1024]{2,1,0:T(2,128)(2,1)} %reshape.883), calls=%async_computation.3 | async-start | bytes 524288 | tf_op jit(solution)/shard_map/all_to_all | solution.py:202
  130.3 1.1 copy-start.11
  130.6 0.9 copy-start.13
  133.2 26.6 %copy-start.1 = (f32[1,16,64,256]{3,2,1,0:T(8,128)}, f32[1,16,64,256]{3,2,1,0:T(8,128)S(1)}, u32[]{:S(2)}) copy-start(f32[1,16,64,256]{3,2,1,0:T(8,128)S(1)} %convolution_bitcast_fusion.2) | copy-start | bytes 3145732
  149.5 6.3 copy-start.3
  162.0 4.0 copy-start.2
  169.9 6.2 copy-start.14
  169.9 7.1 %copy-start.12 = (bf16[1024,1,128]{2,1,0:T(2,128)(2,1)S(1)}, bf16[1024,1,128]{2,1,0:T(2,128)(2,1)}, u32[]{:S(2)}) copy-start(bf16[1024,1,128]{2,1,0:T(2,128)(2,1)} %copy-done.11) | copy-start | bytes 786436
  194.4 60.0 %copy-start.10 = (f32[16,64,256]{2,1,0:T(8,128)S(1)}, f32[16,64,256]{2,1,0:T(8,128)}, u32[]{:S(2)}) copy-start(f32[16,64,256]{2,1,0:T(8,128)} %get-tuple-element.447) | copy-start | bytes 3145732
  245.9 85.7 %all-to-all-start.2 = ((bf16[64,2,1024]{2,1,0:T(2,128)(2,1)}), bf16[64,2,1024]{2,1,0:T(2,128)(2,1)S(1)}, u32[]{:S(2)}, u32[]{:S(2)}) async-start(bf16[64,2,1024]{2,1,0:T(2,128)(2,1)} %reshape.881), calls=%async_computation.2 | async-start | bytes 524288 | tf_op jit(solution)/shard_map/all_to_all | solution.py:215
  261.7 3.6 copy-start.15
  262.6 5.3 copy-start.16
  280.3 64.8 %copy-start = (f32[16,64,256]{2,1,0:T(8,128)S(1)}, f32[16,64,256]{2,1,0:T(8,128)}, u32[]{:S(2)}) copy-start(f32[16,64,256]{2,1,0:T(8,128)} %get-tuple-element.632) | copy-start | bytes 3145732
  280.3 64.8 %copy-start.35 = (f32[16,16]{1,0:T(8,128)S(1)}, f32[16,16]{1,0:T(8,128)}, u32[]{:S(2)}) copy-start(f32[16,16]{1,0:T(8,128)} %custom-call.2) | copy-start | bytes 3076
  280.3 64.8 %copy-start.36 = (f32[16,16]{1,0:T(8,128)S(1)}, f32[16,16]{1,0:T(8,128)}, u32[]{:S(2)}) copy-start(f32[16,16]{1,0:T(8,128)} %custom-call.3) | copy-start | bytes 3076
  331.6 156.5 %all-to-all-start.4 = ((bf16[64,2,1024]{2,1,0:T(2,128)(2,1)}), bf16[64,2,1024]{2,1,0:T(2,128)(2,1)}, u32[]{:S(2)}, u32[]{:S(2)}) async-start(bf16[64,2,1024]{2,1,0:T(2,128)(2,1)} %reshape.885), calls=%async_computation.4 | async-start | bytes 524288 | tf_op jit(solution)/shard_map/all_to_all | solution.py:216
  488.1 32.2 %all-to-all-start.5 = ((bf16[64,2,1024]{2,1,0:T(2,128)(2,1)}), bf16[64,2,1024]{2,1,0:T(2,128)(2,1)S(1)}, u32[]{:S(2)}, u32[]{:S(2)}) async-start(bf16[64,2,1024]{2,1,0:T(2,128)(2,1)} %reshape.887), calls=%async_computation.5 | async-start | bytes 524288 | tf_op jit(solution)/shard_map/all_to_all | solution.py:217
  501.5 18.0 %copy-start.5 = (f32[1,1024,130]{2,1,0:T(8,128)S(1)}, f32[1,1024,130]{2,1,0:T(8,128)}, u32[]{:S(2)}) copy-start(f32[1,1024,130]{2,1,0:T(8,128)} %copy-done.4) | copy-start | bytes 1597444
  520.3 15.9 %copy-start.7 = (f32[1,1024,130]{2,1,0:T(8,128)S(1)}, f32[1,1024,130]{2,1,0:T(8,128)}, u32[]{:S(2)}) copy-start(f32[1,1024,130]{2,1,0:T(8,128)} %copy-done.6) | copy-start | bytes 1597444
  528.0 9.1 %copy-start.9 = (f32[1,1024,130]{2,1,0:T(8,128)S(1)}, f32[1,1024,130]{2,1,0:T(8,128)}, u32[]{:S(2)}) copy-start(f32[1,1024,130]{2,1,0:T(8,128)} %copy-done.8) | copy-start | bytes 1597444
  528.0 9.1 %copy-start.18 = (bf16[1,1024,128]{2,1,0:T(8,128)(2,1)S(1)}, bf16[1,1024,128]{2,1,0:T(8,128)(2,1)}, u32[]{:S(2)}) copy-start(bf16[1,1024,128]{2,1,0:T(8,128)(2,1)} %param.14) | copy-start | bytes 786436
  536.0 96.0 %copy-start.28 = (f32[1,1,1024]{2,1,0:T(1,128)S(1)}, f32[1,1,1024]{2,1,0:T(1,128)}, u32[]{:S(2)}) copy-start(f32[1,1,1024]{2,1,0:T(1,128)} %copy-done.27) | copy-start | bytes 12292
  536.0 96.0 %copy-start.30 = (f32[1,1,1024]{2,1,0:T(1,128)S(1)}, f32[1,1,1024]{2,1,0:T(1,128)}, u32[]{:S(2)}) copy-start(f32[1,1,1024]{2,1,0:T(1,128)} %copy-done.29) | copy-start | bytes 12292
  536.0 96.0 %copy-start.32 = (f32[1,1,1024]{2,1,0:T(1,128)S(1)}, f32[1,1,1024]{2,1,0:T(1,128)}, u32[]{:S(2)}) copy-start(f32[1,1,1024]{2,1,0:T(1,128)} %copy-done.31) | copy-start | bytes 12292
  537.0 99.4 %copy-start.22 = (f32[1,1,1024]{2,1,0:T(1,128)S(1)}, f32[1,1,1024]{2,1,0:T(1,128)}, u32[]{:S(2)}) copy-start(f32[1,1,1024]{2,1,0:T(1,128)} %copy-done.21) | copy-start | bytes 12292
  537.1 99.4 %copy-start.24 = (f32[1,1,1024]{2,1,0:T(1,128)S(1)}, f32[1,1,1024]{2,1,0:T(1,128)}, u32[]{:S(2)}) copy-start(f32[1,1,1024]{2,1,0:T(1,128)} %copy-done.23) | copy-start | bytes 12292
  537.1 99.4 %copy-start.26 = (f32[1,1,1024]{2,1,0:T(1,128)S(1)}, f32[1,1,1024]{2,1,0:T(1,128)}, u32[]{:S(2)}) copy-start(f32[1,1,1024]{2,1,0:T(1,128)} %copy-done.25) | copy-start | bytes 12292
  615.1 16.8 %collective-permute-start.5 = (bf16[1,1024,2]{2,1,0:T(8,128)(2,1)S(1)}, bf16[1,1024,2]{2,1,0:T(8,128)(2,1)S(1)}, u32[]{:S(2)}, u32[]{:S(2)}) collective-permute-start(bf16[1,1024,2]{2,1,0:T(8,128)(2,1)S(1)} %bitcast.321), channel_id=1, source_target_pairs={{1,0},{2,1},{3,2},{4,3},{5,4},{6,5},{7,6},{8,7},{9,8},{10,9},{11,1... | collective-permute-start | bytes 12296 | tf_op jit(solution)/shard_map/ppermute | solution.py:14
  617.6 18.8 %collective-permute-start.4 = (bf16[1,1024,2]{2,1,0:T(8,128)(2,1)S(1)}, bf16[1,1024,2]{2,1,0:T(8,128)(2,1)S(1)}, u32[]{:S(2)}, u32[]{:S(2)}) collective-permute-start(bf16[1,1024,2]{2,1,0:T(8,128)(2,1)S(1)} %bitcast.318), channel_id=1, source_target_pairs={{1,0},{2,1},{3,2},{4,3},{5,4},{6,5},{7,6},{8,7},{9,8},{10,9},{11,1... | collective-permute-start | bytes 12296 | tf_op jit(solution)/shard_map/ppermute | solution.py:14
  621.1 16.9 %collective-permute-start.3 = (bf16[1,1024,2]{1,2,0:T(2,128)(2,1)S(1)}, bf16[1,1024,2]{1,2,0:T(2,128)(2,1)S(1)}, u32[]{:S(2)}, u32[]{:S(2)}) collective-permute-start(bf16[1,1024,2]{1,2,0:T(2,128)(2,1)S(1)} %copy.217), channel_id=1, source_target_pairs={{1,0},{2,1},{3,2},{4,3},{5,4},{6,5},{7,6},{8,7},{9,8},{10,9},{11,1... | collective-permute-start | bytes 12296 | tf_op jit(solution)/shard_map/ppermute | solution.py:14
where the time goes:
time: 652 us; the launch traced here: 640 us
  other arithmetic  289 us (44%)
  local copies, waits for them, and re-layouts  99 us (15%)
  starting transfers between devices  91.3 us (14%)
  blocking collectives  85.8 us (13%)
  matrix products  48.9 us (8%)
  waiting for transfers between devices  22.9 us (4%)
    unnamed x9, other arithmetic  146 us
    psum x1, blocking collectives, per_device(): tap_total = lax.psum(tap_part, ('dp', 'context'))  75.4 us
    unnamed x93, local copies, waits for them, and re-layouts  48.6 us
    dot_general x16, matrix products, along_cols(): jnp.einsum('bckm,mj->bckj', array, table, precision=HIGHEST_PRECISION)  38.5 us
    reduce_sum x16, other arithmetic, one_mode(): jnp.sum(adj_re * tangents[0] + adj_im * tangents[1], axis=(1, 2))  35.3 us
    ppermute x6, waiting for transfers between devices, passed_along(): return lax.ppermute(x, axis, pairs)  18.1 us
    ppermute x6, starting transfers between devices, passed_along(): return lax.ppermute(x, axis, pairs)  18 us
    add x16, other arithmetic, add_mode(): carry[1] + weight_col * resp_im  16.5 us
  transfers between devices with their start and end apart: 12, of which 4 were waited for; matrix products, arithmetic and copies ran while one was open for 47% of the time, Pallas kernels for 0%

commit v1 on v0

v1 whole, which is shorter than its diff:
```python
import functools
import math

import jax
import jax.numpy as jnp
from jax import lax
from jax.experimental import pallas as pl
from jax.experimental.pallas import tpu as pltpu
from jax.sharding import PartitionSpec as P

F32 = jnp.float32
BF16 = jnp.bfloat16
HIGHEST = lax.Precision.HIGHEST
LANES = 128
SUBS = 8
GROUP = 8


def rounded(x):
    return x.astype(BF16).astype(F32)


def owner_kernel(
    own, modes, taps, steps, scale,
    q_ref, k_ref, v_ref, c_ref, table_ref,
    out_ref, dq_ref, dk_ref, dv_ref, small_ref,
    xq, xk, xv, xc, qs, ks, vs, gs, us, ys, ss, aq, ak, av,
    tab, lst, pst, adj, qacc, racc, tacc,
):
    lane = lax.broadcasted_iota(jnp.int32, (SUBS, LANES), 1)
    sub = lax.broadcasted_iota(jnp.int32, (SUBS, LANES), 0)
    per_row = LANES // own
    chunk = sub * per_row + lane // own
    chunks = SUBS * per_row

    def later(x, by):
        if by < per_row:
            turned = pltpu.roll(x, own * by, 1)
            x = jnp.where(lane >= own * by, turned, pltpu.roll(turned, 1, 0))
        else:
            x = pltpu.roll(x, by // per_row, 0)
        return jnp.where(chunk >= by, x, 0.0)

    def earlier(x, by):
        if by < per_row:
            turned = pltpu.roll(x, LANES - own * by, 1)
            x = jnp.where(lane < LANES - own * by, turned, pltpu.roll(turned, SUBS - 1, 0))
        else:
            x = pltpu.roll(x, SUBS - by // per_row, 0)
        return jnp.where(chunk < chunks - by, x, 0.0)

    def at(t):
        return pl.ds(pl.multiple_of(t * SUBS, SUBS), SUBS)

    spread = (
        lax.broadcasted_iota(jnp.int32, (own, LANES), 0)
        == lax.broadcasted_iota(jnp.int32, (own, LANES), 1) % own
    ).astype(F32)
    rows = jnp.dot(table_ref[...], spread, precision=HIGHEST, preferred_element_type=F32)
    n_rows = 3 * modes + 3 * taps
    for row in range(n_rows):
        tab[pl.ds(row * SUBS, SUBS), :] = jnp.broadcast_to(rows[row : row + 1, :], (SUBS, LANES))

    def entry(row):
        return tab[pl.ds(row * SUBS, SUBS), :]

    ones = (
        lax.broadcasted_iota(jnp.int32, (LANES, LANES), 0)
        == lax.broadcasted_iota(jnp.int32, (LANES, LANES), 1)
    ).astype(BF16)

    def flipped(x):
        return lax.dot_general(ones, x, (((1,), (1,)), ((), ())), preferred_element_type=F32)

    reach = taps - 1
    head = reach * SUBS
    for src, dst in ((q_ref, xq), (k_ref, xk), (v_ref, xv), (c_ref, xc)):
        for i in range(SUBS):
            dst[pl.ds(head + i, steps, stride=SUBS), :] = flipped(src[pl.ds(i * LANES, LANES), :])
    for x in (xq, xk, xv):
        for j in range(reach):
            x[pl.ds(j * SUBS, SUBS), :] = later(x[pl.ds(head + (steps - reach + j) * SUBS, SUBS), :], 1)

    def tap(stream, j):
        return entry(3 * modes + stream * taps + j)

    def filtered(x, stream, t):
        total = tap(stream, 0) * x[at(t + reach), :]
        for j in range(1, taps):
            total = total + tap(stream, j) * x[at(t + reach - j), :]
        return rounded(total)

    def features(t, carry):
        query, key, value = filtered(xq, 0, t), filtered(xk, 1, t), filtered(xv, 2, t)
        qs[at(t), :] = query
        ks[at(t), :] = key
        vs[at(t), :] = value
        gs[at(t), :] = rounded(key * value)
        us[at(t), :] = rounded(xc[at(t + reach), :] * query)
        return carry

    lax.fori_loop(0, steps, features, 0, unroll=4)

    zero = jnp.zeros((SUBS, LANES), F32)

    def ends(t, carry):
        gated = gs[at(t), :]
        upstream = us[at(steps - 1 - t), :]
        ahead, back = carry
        decays = [entry(m) for m in range(modes)]
        return (
            tuple(decays[m] * ahead[m] + gated for m in range(modes)),
            tuple(decays[m] * back[m] + upstream for m in range(modes)),
        )

    zeros = tuple(zero for _ in range(modes))
    ahead, back = lax.fori_loop(0, steps, ends, (zeros, zeros), unroll=2)
    for m in range(modes):
        lst[pl.ds(m * SUBS, SUBS), :] = ahead[m]
        pst[pl.ds(m * SUBS, SUBS), :] = back[m]

    def chain(m, carry):
        power = tab[at(m + n_rows), :]
        total, behind = lst[at(m), :], pst[at(m), :]
        by = 1
        while by < chunks:
            total = total + power * later(total, by)
            behind = behind + power * earlier(behind, by)
            power = power * power
            by *= 2
        lst[at(m), :] = later(total, 1)
        pst[at(m), :] = earlier(behind, 1)
        return carry

    for m in range(modes):
        decay = entry(modes + m)
        tab[pl.ds((n_rows + m) * SUBS, SUBS), :] = jnp.exp(decay * (-float(steps)))
    lax.fori_loop(0, modes, chain, 0)

    for group in range(0, modes, GROUP):
        members = range(group, group + GROUP)

        def backward(i, carry):
            t = steps - 1 - i
            upstream = us[at(t), :]
            total = zero if group == 0 else ss[at(t), :]
            new = []
            for n, m in enumerate(members):
                state = entry(m) * carry[n] + upstream
                adj[at(t * GROUP + n), :] = state
                total = total + entry(2 * modes + m) * state
                new.append(state)
            ss[at(t), :] = total
            return tuple(new)

        lax.fori_loop(0, steps, backward, tuple(pst[pl.ds(m * SUBS, SUBS), :] for m in members), unroll=2)

        def forward(t, carry):
            states, firsts, seconds = carry
            gated = gs[at(t), :]
            upstream = us[at(t), :]
            total = zero if group == 0 else ys[at(t), :]
            new_s, new_f, new_r = [], [], []
            for n, m in enumerate(members):
                new_r.append(seconds[n] + states[n] * adj[at(t * GROUP + n), :])
                state = entry(m) * states[n] + gated
                new_f.append(firsts[n] + upstream * state)
                total = total + entry(2 * modes + m) * state
                new_s.append(state)
            ys[at(t), :] = total
            return tuple(new_s), tuple(new_f), tuple(new_r)

        few = tuple(zero for _ in members)
        _, firsts, seconds = lax.fori_loop(
            0, steps, forward, (tuple(lst[pl.ds(m * SUBS, SUBS), :] for m in members), few, few), unroll=2
        )
        for n, m in enumerate(members):
            qacc[pl.ds(m, 1), :] = jnp.sum(firsts[n], axis=0, keepdims=True)
            racc[pl.ds(m, 1), :] = jnp.sum(seconds[n], axis=0, keepdims=True)

    def products(t, carry):
        mixed = rounded(ys[at(t), :])
        source = rounded(ss[at(t), :])
        query = qs[at(t), :]
        ys[at(t), :] = query * mixed
        grads = (
            rounded(xc[at(t + reach), :] * mixed),
            rounded(source * vs[at(t), :]),
            rounded(source * ks[at(t), :]),
        )
        new = []
        for stream, (grad, ref, x) in enumerate(zip(grads, (aq, ak, av), (xq, xk, xv))):
            ref[at(t), :] = grad
            for j in range(taps):
                new.append(carry[stream * taps + j] + grad * x[at(t + reach - j), :])
        return tuple(new)

    tacc[...] = jnp.zeros(tacc.shape, F32)
    sums = lax.fori_loop(0, steps, products, tuple(zero for _ in range(3 * taps)), unroll=2)
    for n in range(3 * taps):
        tacc[pl.ds(n, 1), :] = jnp.sum(sums[n], axis=0, keepdims=True)

    for a in (aq, ak, av):
        for j in range(reach):
            a[pl.ds((steps + j) * SUBS, SUBS), :] = earlier(a[pl.ds(j * SUBS, SUBS), :], 1)

    def gradients(t, carry):
        for stream, (a, dst) in enumerate(((aq, gs), (ak, us), (av, ss))):
            total = tap(stream, 0) * a[at(t), :]
            for j in range(1, taps):
                total = total + tap(stream, j) * a[at(t + j), :]
            dst[at(t), :] = total
        return carry

    lax.fori_loop(0, steps, gradients, 0, unroll=4)
    for src, dst in ((ys, out_ref), (gs, dq_ref), (us, dk_ref), (ss, dv_ref)):
        for i in range(SUBS):
            part = src[pl.ds(i, steps, stride=SUBS), :].astype(BF16)
            dst[pl.ds(i * LANES, LANES), :] = flipped(part).astype(BF16)

    def over_chunks(x):
        by = own
        while by < LANES:
            x = x + pltpu.roll(x, by, 1)
            by *= 2
        return x

    first = over_chunks(qacc[...])
    second = over_chunks(racc[...]) * rows[:modes]
    decay = rows[modes : 2 * modes]
    weighted = rows[2 * modes : 3 * modes]
    size = table_sizes(table_ref, n_rows, modes, spread)
    damp = rows[:modes] * rows[:modes]
    small_ref[pl.ds(0, modes), :] = scale * size * first
    bend = residue_part(table_ref, n_rows, modes, spread) * (damp / size) * first - weighted * second
    small_ref[pl.ds(modes, modes), :] = scale * decay * bend
    small_ref[pl.ds(2 * modes, tacc.shape[0]), :] = scale * over_chunks(tacc[...])


def table_sizes(table_ref, start, modes, spread):
    part = table_ref[pl.ds(TABLE_EXTRA, modes), :]
    return jnp.dot(part, spread, precision=HIGHEST, preferred_element_type=F32)


def residue_part(table_ref, start, modes, spread):
    part = table_ref[pl.ds(TABLE_EXTRA + modes, modes), :]
    return jnp.dot(part, spread, precision=HIGHEST, preferred_element_type=F32)


TABLE_EXTRA = 64


def per_device(queries, key_stream, value_stream, cotangent, short_taps, residues, decay_rates):
    channels, steps = queries.shape[1], queries.shape[2]
    own, modes = residues.shape
    taps = short_taps.shape[1]
    owners = lax.axis_size("context")
    scale = 1.0 / math.sqrt(queries.shape[0] * lax.axis_size("dp") * steps * owners)
    me = lax.axis_index("context")

    mine = [
        lax.all_to_all(x.reshape(channels, steps), "context", 0, 0, tiled=True)
        for x in (queries, key_stream, value_stream, cotangent)
    ]
    rates = decay_rates.T
    size = jnp.sqrt(-jnp.expm1(-2.0 * rates))
    own_taps = lax.dynamic_slice(short_taps.reshape(3 * taps, channels), (0, me * own), (3 * taps, own))
    n_rows = 3 * modes + 3 * taps
    table = jnp.concatenate(
        [
            jnp.exp(-rates),
            rates,
            residues.T * size,
            own_taps,
            jnp.zeros((TABLE_EXTRA - n_rows, own), F32),
            size,
            residues.T,
        ]
    )
    wide = jax.ShapeDtypeStruct((channels, steps), BF16)
    line = steps * SUBS
    reach = taps - 1
    vm = pltpu.VMEM
    tap_rows = 16
    results = pl.pallas_call(
        functools.partial(owner_kernel, own, modes, taps, steps, scale),
        out_shape=[wide] * 4 + [jax.ShapeDtypeStruct((2 * modes + tap_rows, LANES), F32)],
        in_specs=[pl.BlockSpec(memory_space=vm)] * 5,
        out_specs=[pl.BlockSpec(memory_space=vm)] * 5,
        scratch_shapes=[vm((line + reach * SUBS, LANES), F32)] * 4
        + [vm((line, LANES), F32)] * 7
        + [vm((line + reach * SUBS, LANES), F32)] * 3
        + [
            vm(((n_rows + modes) * SUBS, LANES), F32),
            vm((modes * SUBS, LANES), F32),
            vm((modes * SUBS, LANES), F32),
            vm((line * GROUP, LANES), F32),
            vm((modes, LANES), F32),
            vm((modes, LANES), F32),
            vm((tap_rows, LANES), F32),
        ],
        compiler_params=pltpu.CompilerParams(vmem_limit_bytes=48 * 1024 * 1024),
    )(*mine, table)
    small = results[4][:, :own]
    for by in (1, 2):
        small = small + lax.ppermute(small, "dp", [(i, i ^ by) for i in range(lax.axis_size("dp"))])
    outs = [
        lax.all_to_all(x, "context", 0, 0, tiled=True).reshape(queries.shape) for x in results[:4]
    ]
    flat = jnp.pad(small[2 * modes : 2 * modes + 3 * taps].reshape(-1), (0, 2 * LANES - 3 * taps * own))
    shared = lax.all_to_all(
        jnp.broadcast_to(flat.reshape(1, 2, LANES), (owners, 2, LANES)), "context", 0, 0, tiled=True
    )
    tap_total = shared.reshape(owners, 2 * LANES)[:, : 3 * taps * own].reshape(owners, 3, taps, own)
    tap_total = tap_total.transpose(1, 2, 0, 3).reshape(3, taps, channels)
    return (*outs, tap_total, small[:modes].T, small[modes : 2 * modes].T)


def solution(mesh):
    stream = P("dp", None, "context")
    in_specs = (stream,) * 4 + (P(), P("context", None), P("context", None))
    out_specs = (stream,) * 4 + (P(), P("context", None), P("context", None))
    return jax.shard_map(per_device, mesh=mesh, in_specs=in_specs, out_specs=out_specs, check_vma=False)
```

time: 652 us -> 199 us (0.31)
  the two profiles are of different devices: /device:TPU:230 before, /device:TPU:32 now
where the time goes in v1:
time: 199 us; the launch traced here: 198 us
  blocking collectives  136 us (68%)
  waiting for transfers between devices  26.7 us (13%)
  Pallas kernels  16.9 us (8%)
  starting transfers between devices  10.7 us (5%)
  local copies, waits for them, and re-layouts  6.89 us (3%)
    all_to_all x3, blocking collectives, per_device(): lax.all_to_all(x.reshape(channels, steps), 'context', 0, 0, tiled=True)  66.2 us
    all_to_all x3, blocking collectives, per_device(): lax.all_to_all(x, 'context', 0, 0, tiled=True).reshape(queries.shape)  53.7 us
    pallas_call x1, Pallas kernels, per_device(): pl.pallas_call(functools.partial(owner_kernel, own, modes, taps, steps, s...  16.9 us
    all_to_all x1, blocking collectives, per_device(): lax.all_to_all(jnp.broadcast_to(flat.reshape(1, 2, LANES), (owners, 2, LA...  16.2 us
    all_to_all x1, waiting for transfers between devices, per_device(): lax.all_to_all(x.reshape(channels, steps), 'context', 0, 0, tiled=True)  11.6 us
    all_to_all x1, waiting for transfers between devices, per_device(): lax.all_to_all(x, 'context', 0, 0, tiled=True).reshape(queries.shape)  10.8 us
    unnamed x18, local copies, waits for them, and re-layouts  5.61 us
    all_to_all x1, starting transfers between devices, per_device(): lax.all_to_all(x.reshape(channels, steps), 'context', 0, 0, tiled=True)  5.03 us
  transfers between devices with their start and end apart: 4, of which 4 were waited for; matrix products, arithmetic and copies ran while one was open for 1% of the time, Pallas kernels for 0%

profile of v1, /device:TPU:32, one launch (start us, length us, event | category | flops | bytes accessed | tf_op | source)
XLA Modules:
  0.0 198.0 jit_solution(365030803131835283)
XLA Ops:
  0.6 0.0 copy-start
  0.6 29.0 %all_to_all.85 = bf16[64,16,128]{2,1,0:T(8,128)(2,1)S(1)} all-to-all(bf16[64,16,128]{2,1,0:T(8,128)(2,1)} %bitcast.50), channel_id=1, replica_groups=mesh['dp'=4,'context'=64] {'context'}, dimensions={0} | all-to-all | bytes 524288 | tf_op jit(solution)/shard_map/all_to_all | solution.py:262
  29.6 0.0 copy-done
  29.6 0.0 copy-start.1
  29.6 18.8 %all_to_all.86 = bf16[64,16,128]{2,1,0:T(8,128)(2,1)S(1)} all-to-all(bf16[64,16,128]{2,1,0:T(8,128)(2,1)S(1)} %bitcast.51), channel_id=1, replica_groups=mesh['dp'=4,'context'=64] {'context'}, dimensions={0} | all-to-all | bytes 524288 | tf_op jit(solution)/shard_map/all_to_all | solution.py:262
  48.4 0.0 copy-done.1
  48.4 18.4 %all_to_all.87 = bf16[64,16,128]{2,1,0:T(8,128)(2,1)S(1)} all-to-all(bf16[64,16,128]{2,1,0:T(8,128)(2,1)S(1)} %bitcast.52), channel_id=1, replica_groups=mesh['dp'=4,'context'=64] {'context'}, dimensions={0} | all-to-all | bytes 524288 | tf_op jit(solution)/shard_map/all_to_all | solution.py:262
  66.8 0.0 copy-start.2
  66.8 5.0 %all-to-all-start.3 = ((bf16[64,16,128]{2,1,0:T(8,128)(2,1)}), bf16[64,16,128]{2,1,0:T(8,128)(2,1)S(1)}, u32[]{:S(2)}, u32[]{:S(2)}) async-start(bf16[64,16,128]{2,1,0:T(8,128)(2,1)} %bitcast.6), calls=%async_computation.3 | async-start | bytes 524288 | tf_op jit(solution)/shard_map/all_to_all | solution.py:262
  71.9 0.0 copy-start.3
  71.9 0.7 copy-done.3
  72.6 0.0 copy-start.4
  72.6 0.1 copy.36
  72.7 0.6 copy-done.4
  73.3 0.1 copy.35
  73.3 0.0 copy-done.2
  73.4 0.1 constant_dynamic-slice_fusion
  73.5 11.6 %all-to-all-done.3 = bf16[64,16,128]{2,1,0:T(8,128)(2,1)S(1)} async-done(((bf16[64,16,128]{2,1,0:T(8,128)(2,1)}), bf16[64,16,128]{2,1,0:T(8,128)(2,1)S(1)}, u32[]{:S(2)}, u32[]{:S(2)}) %all-to-all-start.3) | async-done | bytes 262176 | tf_op jit(solution)/shard_map/all_to_all | solution.py:262
  85.1 16.9 %shard_map.126 = (bf16[1024,128]{1,0:T(8,128)(2,1)S(1)}, bf16[1024,128]{1,0:T(8,128)(2,1)S(1)}, bf16[1024,128]{1,0:T(8,128)(2,1)S(1)}, bf16[1024,128]{1,0:T(8,128)(2,1)}, f32[48,128]{1,0:T(8,128)S(1)}) custom-call(bf16[1024,128]{1,0:T(8,128)(2,1)S(1)} %bitcast.36, bf16[1024,128]{1,0:T(8,128)(2,1)S(1)} %bitcast.37, bf16[1024,128]{1,0:T(8,128)(2,1)S(1)} %bitcast.38, ...), custom_call_target="tpu_custom_call" | custom-call | tf_op jit(solution)/shard_map/pallas_call | solution.py:285
  102.0 0.0 collective-permute-start
  102.0 1.2 collective-permute-done
  103.2 0.8 collective-permute-start.1
  104.0 3.1 %collective-permute-done.1 = f32[48,16]{1,0:T(8,128)S(1)} collective-permute-done((f32[48,16]{1,0:T(8,128)S(1)}, f32[48,16]{1,0:T(8,128)S(1)}, u32[]{:S(2)}, u32[]{:S(2)}) %collective-permute-start.1) | collective-permute-done | bytes 3104 | tf_op jit(solution)/shard_map/ppermute | solution.py:306
  107.0 0.1 reshape.76
  107.2 16.2 %all_to_all.88 = f32[64,2,128]{2,1,0:T(2,128)S(1)} all-to-all(f32[64,2,128]{2,1,0:T(2,128)S(1)} %broadcast_in_dim.12), channel_id=1, replica_groups=mesh['dp'=4,'context'=64] {'context'}, dimensions={0} | all-to-all | bytes 131072 | tf_op jit(solution)/shard_map/all_to_all | solution.py:311
  123.3 17.8 %all_to_all.89 = bf16[64,16,128]{2,1,0:T(8,128)(2,1)S(1)} all-to-all(bf16[64,16,128]{2,1,0:T(8,128)(2,1)S(1)} %bitcast.42), channel_id=1, replica_groups=mesh['dp'=4,'context'=64] {'context'}, dimensions={0} | all-to-all | bytes 524288 | tf_op jit(solution)/shard_map/all_to_all | solution.py:308
  141.1 17.9 %all_to_all.90 = bf16[64,16,128]{2,1,0:T(8,128)(2,1)S(1)} all-to-all(bf16[64,16,128]{2,1,0:T(8,128)(2,1)S(1)} %bitcast.41), channel_id=1, replica_groups=mesh['dp'=4,'context'=64] {'context'}, dimensions={0} | all-to-all | bytes 524288 | tf_op jit(solution)/shard_map/all_to_all | solution.py:308
  159.1 17.9 %all_to_all.91 = bf16[64,16,128]{2,1,0:T(8,128)(2,1)S(1)} all-to-all(bf16[64,16,128]{2,1,0:T(8,128)(2,1)S(1)} %bitcast.40), channel_id=1, replica_groups=mesh['dp'=4,'context'=64] {'context'}, dimensions={0} | all-to-all | bytes 524288 | tf_op jit(solution)/shard_map/all_to_all | solution.py:308
  177.0 4.9 %all-to-all-start.7 = ((bf16[64,16,128]{2,1,0:T(8,128)(2,1)}), bf16[64,16,128]{2,1,0:T(8,128)(2,1)S(1)}, u32[]{:S(2)}, u32[]{:S(2)}) async-start(bf16[64,16,128]{2,1,0:T(8,128)(2,1)} %bitcast.16), calls=%async_computation.7 | async-start | bytes 524288 | tf_op jit(solution)/shard_map/all_to_all | solution.py:308
  182.0 0.7 copy.40
  182.7 0.7 copy.39
  183.3 0.1 copy.37
  183.4 0.1 copy.38
  183.6 0.8 reshape.79
  184.4 10.8 %all-to-all-done.7 = bf16[64,16,128]{2,1,0:T(8,128)(2,1)S(1)} async-done(((bf16[64,16,128]{2,1,0:T(8,128)(2,1)}), bf16[64,16,128]{2,1,0:T(8,128)(2,1)S(1)}, u32[]{:S(2)}, u32[]{:S(2)}) %all-to-all-start.7) | async-done | bytes 262176 | tf_op jit(solution)/shard_map/all_to_all | solution.py:308
  195.2 0.7 copy.45
  195.9 0.7 copy.46
  196.6 0.7 copy.47
  197.3 0.7 copy.48
  (11 shorter events, 0.1 us)
Async XLA Ops:
  0.6 29.0 %copy-start = (bf16[1,1024,128]{2,1,0:T(8,128)(2,1)S(1)}, bf16[1,1024,128]{2,1,0:T(8,128)(2,1)}, u32[]{:S(2)}) copy-start(bf16[1,1024,128]{2,1,0:T(8,128)(2,1)} %param.8) | copy-start | bytes 786436
  29.6 18.8 %copy-start.1 = (bf16[1,1024,128]{2,1,0:T(8,128)(2,1)S(1)}, bf16[1,1024,128]{2,1,0:T(8,128)(2,1)}, u32[]{:S(2)}) copy-start(bf16[1,1024,128]{2,1,0:T(8,128)(2,1)} %param.9) | copy-start | bytes 786436
  66.8 6.5 %copy-start.2 = (f32[3,3,1024]{2,1,0:T(4,128)S(1)}, f32[3,3,1024]{2,1,0:T(4,128)}, u32[]{:S(2)}) copy-start(f32[3,3,1024]{2,1,0:T(4,128)} %param.11) | copy-start | bytes 110596
  66.8 18.3 %all-to-all-start.3 = ((bf16[64,16,128]{2,1,0:T(8,128)(2,1)}), bf16[64,16,128]{2,1,0:T(8,128)(2,1)S(1)}, u32[]{:S(2)}, u32[]{:S(2)}) async-start(bf16[64,16,128]{2,1,0:T(8,128)(2,1)} %bitcast.6), calls=%async_computation.3 | async-start | bytes 524288 | tf_op jit(solution)/shard_map/all_to_all | solution.py:262
  71.9 0.7 copy-start.3
  72.6 0.7 copy-start.4
  102.0 1.2 collective-permute-start
  103.2 3.8 %collective-permute-start.1 = (f32[48,16]{1,0:T(8,128)S(1)}, f32[48,16]{1,0:T(8,128)S(1)}, u32[]{:S(2)}, u32[]{:S(2)}) collective-permute-start(f32[48,16]{1,0:T(8,128)S(1)} %slice_add_fusion), channel_id=1, source_target_pairs={{0,128},{64,192},{128,0},{192,64},{1,129},{65,193},{129,1},{193,65... | collective-permute-start | bytes 9224 | tf_op jit(solution)/shard_map/ppermute | solution.py:306
  177.0 18.2 %all-to-all-start.7 = ((bf16[64,16,128]{2,1,0:T(8,128)(2,1)}), bf16[64,16,128]{2,1,0:T(8,128)(2,1)S(1)}, u32[]{:S(2)}, u32[]{:S(2)}) async-start(bf16[64,16,128]{2,1,0:T(8,128)(2,1)} %bitcast.16), calls=%async_computation.7 | async-start | bytes 524288 | tf_op jit(solution)/shard_map/all_to_all | solution.py:308

commit v2 on v1

--- a/solution.py
+++ b/solution.py
@@ -234,7 +234,13 @@
     small_ref[pl.ds(0, modes), :] = scale * size * first
     bend = residue_part(table_ref, n_rows, modes, spread) * (damp / size) * first - weighted * second
     small_ref[pl.ds(modes, modes), :] = scale * decay * bend
-    small_ref[pl.ds(2 * modes, tacc.shape[0]), :] = scale * over_chunks(tacc[...])
+    total_taps = scale * over_chunks(tacc[...])
+    part = lax.broadcasted_iota(jnp.int32, (1, LANES), 1) // own
+    packed = jnp.zeros((SUBS, LANES), F32)
+    for n in range(3 * taps):
+        spot = (part == n % per_row) & (sub == n // per_row)
+        packed = jnp.where(spot, total_taps[n : n + 1, :], packed)
+    small_ref[pl.ds(2 * modes, SUBS), :] = packed
 
 
 def table_sizes(table_ref, start, modes, spread):
@@ -248,6 +254,128 @@
 
 
 TABLE_EXTRA = 64
+
+
+MESH = pl.DeviceIdType.MESH
+
+
+def greet(axis, peers, me):
+    barrier = pltpu.get_barrier_semaphore()
+
+    def signal(step, carry):
+        pl.semaphore_signal(barrier, inc=1, device_id={axis: lax.rem(me + step, peers)}, device_id_type=MESH)
+        return carry
+
+    lax.fori_loop(1, peers, signal, 0)
+    return barrier
+
+
+def exchange(own, peers, me, sources, targets, send_sem, recv_sem):
+    def piece(i):
+        return pl.ds(pl.multiple_of(i * own, own), own)
+
+    def send(step, carry):
+        peer = lax.rem(me + step, peers)
+        for n, (source, target) in enumerate(zip(sources, targets)):
+            pltpu.make_async_remote_copy(
+                src_ref=source.at[piece(peer)],
+                dst_ref=target.at[piece(me)],
+                send_sem=send_sem.at[n],
+                recv_sem=recv_sem.at[n],
+                device_id={"context": peer},
+                device_id_type=MESH,
+            ).start()
+        return carry
+
+    lax.fori_loop(1, peers, send, 0)
+
+
+def settle(rows, refs, sem):
+    for n, ref in enumerate(refs):
+        whole = ref.at[pl.ds(0, rows)]
+        pltpu.make_async_copy(whole, whole, sem.at[n]).wait()
+
+
+def keep(own, me, sources, targets, sem):
+    spot = pl.ds(pl.multiple_of(me * own, own), own)
+    copies = [
+        pltpu.make_async_copy(source.at[spot], target.at[spot], sem.at[n])
+        for n, (source, target) in enumerate(zip(sources, targets))
+    ]
+    for copy in copies:
+        copy.start()
+    return copies
+
+
+def inbound_kernel(own, peers, *refs):
+    sources, targets = refs[:4], refs[4:8]
+    send_sem, recv_sem, keep_sem = refs[8:]
+    me = lax.axis_index("context")
+    barrier = greet("context", peers, me)
+    copies = keep(own, me, sources, targets, keep_sem)
+    pl.semaphore_wait(barrier, peers - 1)
+    exchange(own, peers, me, sources, targets, send_sem, recv_sem)
+    for copy in copies:
+        copy.wait()
+    settle(own * (peers - 1), targets, recv_sem)
+    settle(own * (peers - 1), sources, send_sem)
+
+
+def outbound_kernel(own, peers, doubles, rows, used, *refs):
+    sources, small, targets, total, shared = refs[:4], refs[4], refs[5:9], refs[9], refs[10]
+    slots, send_sem, recv_sem, keep_sem, pair_send, pair_recv, tap_send, tap_recv = refs[11:]
+    me = lax.axis_index("context")
+    mine = lax.axis_index("dp")
+    barrier = greet("context", peers, me)
+    greet("dp", doubles, mine)
+    copies = keep(own, me, sources, targets, keep_sem)
+    own_small = pltpu.make_async_copy(small, slots.at[mine], keep_sem.at[4])
+    own_small.start()
+    pl.semaphore_wait(barrier, peers + doubles - 2)
+    pairs = []
+    for step in range(1, doubles):
+        pairs.append(
+            pltpu.make_async_remote_copy(
+                src_ref=small,
+                dst_ref=slots.at[mine],
+                send_sem=pair_send.at[step],
+                recv_sem=pair_recv.at[step],
+                device_id={"dp": lax.rem(mine + step, doubles)},
+                device_id_type=MESH,
+            )
+        )
+    for pair in pairs:
+        pair.start()
+    exchange(own, peers, me, sources, targets, send_sem, recv_sem)
+    own_small.wait()
+    for pair in pairs:
+        pair.wait()
+    total[...] = (slots[0] + slots[1]) + (slots[2] + slots[3])
+    spot = pl.ds(pl.multiple_of(me * SUBS, SUBS), used)
+    taps = total.at[pl.ds(rows, used)]
+    own_taps = pltpu.make_async_copy(taps, shared.at[spot], keep_sem.at[5])
+    own_taps.start()
+
+    def send(step, carry):
+        pltpu.make_async_remote_copy(
+            src_ref=taps,
+            dst_ref=shared.at[spot],
+            send_sem=tap_send,
+            recv_sem=tap_recv,
+            device_id={"context": lax.rem(me + step, peers)},
+            device_id_type=MESH,
+        ).start()
+        return carry
+
+    lax.fori_loop(1, peers, send, 0)
+    for copy in copies:
+        copy.wait()
+    own_taps.wait()
+    settle(own * (peers - 1), targets, recv_sem)
+    settle(own * (peers - 1), sources, send_sem)
+    whole = shared.at[pl.ds(0, used * (peers - 1))]
+    pltpu.make_async_copy(whole, whole, tap_recv).wait()
+    pltpu.make_async_copy(whole, whole, tap_send).wait()
 
 
 def per_device(queries, key_stream, value_stream, cotangent, short_taps, residues, decay_rates):
@@ -258,10 +386,18 @@
     scale = 1.0 / math.sqrt(queries.shape[0] * lax.axis_size("dp") * steps * owners)
     me = lax.axis_index("context")
 
-    mine = [
-        lax.all_to_all(x.reshape(channels, steps), "context", 0, 0, tiled=True)
-        for x in (queries, key_stream, value_stream, cotangent)
-    ]
+    wide = jax.ShapeDtypeStruct((channels, steps), BF16)
+    vm = pltpu.VMEM
+    here = pl.BlockSpec(memory_space=vm)
+    dma = pltpu.SemaphoreType.DMA
+    mine = pl.pallas_call(
+        functools.partial(inbound_kernel, own, owners),
+        out_shape=[wide] * 4,
+        in_specs=[here] * 4,
+        out_specs=[here] * 4,
+        scratch_shapes=[dma((4,)), dma((4,)), dma((4,))],
+        compiler_params=pltpu.CompilerParams(collective_id=0, has_side_effects=True),
+    )(*[x.reshape(channels, steps) for x in (queries, key_stream, value_stream, cotangent)])
     rates = decay_rates.T
     size = jnp.sqrt(-jnp.expm1(-2.0 * rates))
     own_taps = lax.dynamic_slice(short_taps.reshape(3 * taps, channels), (0, me * own), (3 * taps, own))
@@ -277,14 +413,12 @@
             residues.T,
         ]
     )
-    wide = jax.ShapeDtypeStruct((channels, steps), BF16)
     line = steps * SUBS
     reach = taps - 1
-    vm = pltpu.VMEM
     tap_rows = 16
     results = pl.pallas_call(
         functools.partial(owner_kernel, own, modes, taps, steps, scale),
-        out_shape=[wide] * 4 + [jax.ShapeDtypeStruct((2 * modes + tap_rows, LANES), F32)],
+        out_shape=[wide] * 4 + [jax.ShapeDtypeStruct((2 * modes + SUBS, LANES), F32)],
         in_specs=[pl.BlockSpec(memory_space=vm)] * 5,
         out_specs=[pl.BlockSpec(memory_space=vm)] * 5,
         scratch_shapes=[vm((line + reach * SUBS, LANES), F32)] * 4
@@ -301,18 +435,30 @@
         ],
         compiler_params=pltpu.CompilerParams(vmem_limit_bytes=48 * 1024 * 1024),
     )(*mine, table)
-    small = results[4][:, :own]
-    for by in (1, 2):
-        small = small + lax.ppermute(small, "dp", [(i, i ^ by) for i in range(lax.axis_size("dp"))])
-    outs = [
-        lax.all_to_all(x, "context", 0, 0, tiled=True).reshape(queries.shape) for x in results[:4]
-    ]
-    flat = jnp.pad(small[2 * modes : 2 * modes + 3 * taps].reshape(-1), (0, 2 * LANES - 3 * taps * own))
-    shared = lax.all_to_all(
-        jnp.broadcast_to(flat.reshape(1, 2, LANES), (owners, 2, LANES)), "context", 0, 0, tiled=True
-    )
-    tap_total = shared.reshape(owners, 2 * LANES)[:, : 3 * taps * own].reshape(owners, 3, taps, own)
+    used = -(-3 * taps * own // LANES)
+    doubles = lax.axis_size("dp")
+    small_shape = jax.ShapeDtypeStruct((2 * modes + SUBS, LANES), F32)
+    *outs, small, shared = pl.pallas_call(
+        functools.partial(outbound_kernel, own, owners, doubles, 2 * modes, used),
+        out_shape=[wide] * 4 + [small_shape, jax.ShapeDtypeStruct((owners * SUBS, LANES), F32)],
+        in_specs=[here] * 5,
+        out_specs=[here] * 6,
+        scratch_shapes=[
+            vm((doubles,) + small_shape.shape, F32),
+            dma((4,)),
+            dma((4,)),
+            dma((6,)),
+            dma((doubles,)),
+            dma((doubles,)),
+            dma,
+            dma,
+        ],
+        compiler_params=pltpu.CompilerParams(collective_id=1, has_side_effects=True),
+    )(*results)
+    outs = [x.reshape(queries.shape) for x in outs]
+    tap_total = shared.reshape(owners, SUBS * LANES)[:, : 3 * taps * own].reshape(owners, 3, taps, own)
     tap_total = tap_total.transpose(1, 2, 0, 3).reshape(3, taps, channels)
+    small = small[:, :own]
     return (*outs, tap_total, small[:modes].T, small[modes : 2 * modes].T)
 
 

time: 199 us -> 111 us (0.56)
  the two profiles are of different devices: /device:TPU:32 before, /device:TPU:1 now
where the time goes in v2:
time: 111 us; the launch traced here: 110 us
  Pallas kernels  93.1 us (84%)
  local copies, waits for them, and re-layouts  16.2 us (15%)
    pallas_call x1, Pallas kernels, per_device(): pl.pallas_call(functools.partial(outbound_kernel, own, owners, doubles, 2...  38.6 us
    pallas_call x1, Pallas kernels, per_device(): pl.pallas_call(functools.partial(inbound_kernel, own, owners), out_shape=...  38.3 us
    pallas_call x1, Pallas kernels, per_device(): pl.pallas_call(functools.partial(owner_kernel, own, modes, taps, steps, s...  16.2 us
    unnamed x41, local copies, waits for them, and re-layouts  13.4 us

profile of v2, /device:TPU:1, one launch (start us, length us, event | category | flops | bytes accessed | tf_op | source)
XLA Modules:
  0.0 110.1 jit_solution(14105984396002809640)
XLA Ops:
  0.6 0.0 copy-start.14
  0.6 0.0 copy-start.15
  0.7 0.0 copy-start.13
  0.7 0.7 copy-done.14
  1.3 0.1 copy.38
  1.4 0.0 copy-done.15
  1.4 0.1 copy.37
  1.5 0.0 copy-done.13
  1.5 0.1 constant_dynamic-slice_fusion
  1.6 38.3 %shard_map.126 = (bf16[1024,128]{1,0:T(8,128)(2,1)}, bf16[1024,128]{1,0:T(8,128)(2,1)}, bf16[1024,128]{1,0:T(8,128)(2,1)}, bf16[1024,128]{1,0:T(8,128)(2,1)}) custom-call(bf16[1024,128]{1,0:T(8,128)(2,1)} %bitcast.29, bf16[1024,128]{1,0:T(8,128)(2,1)} %bitcast.30, bf16[1024,128]{1,0:T(8,128)(2,1)} %bitcast.31, bf16[1024,128]{1,0:T(8,128)(2,1)} %bitcast.32), custom_call_target="tpu_custom_call" | custom-call | tf_op jit(solution)/shard_map/pallas_call | solution.py:393
  39.9 0.0 copy-start.4
  39.9 0.9 copy-done.4
  40.9 0.0 copy-start.5
  40.9 0.9 copy-done.5
  41.8 0.0 copy-start.6
  41.8 0.9 copy-done.6
  42.8 0.0 copy-start.7
  42.8 0.9 copy-done.7
  43.7 16.2 %shard_map.127 = (bf16[1024,128]{1,0:T(8,128)(2,1)S(1)}, bf16[1024,128]{1,0:T(8,128)(2,1)S(1)}, bf16[1024,128]{1,0:T(8,128)(2,1)S(1)}, bf16[1024,128]{1,0:T(8,128)(2,1)S(1)}, f32[40,128]{1,0:T(8,128)S(1)}) custom-call(bf16[1024,128]{1,0:T(8,128)(2,1)S(1)} %copy-done.4, bf16[1024,128]{1,0:T(8,128)(2,1)S(1)} %copy-done.5, bf16[1024,128]{1,0:T(8,128)(2,1)S(1)} %copy-done.6, ...), custom_call_target="tpu_custom_call" | custom-call | tf_op jit(solution)/shard_map/pallas_call | solution.py:419
  60.0 0.0 copy-start
  60.0 0.7 copy-done
  60.7 0.0 copy-start.1
  60.7 0.7 copy-done.1
  61.4 0.0 copy-start.2
  61.4 0.7 copy-done.2
  62.1 0.0 copy-start.3
  62.1 0.7 copy-done.3
  62.8 0.0 copy-start.8
  62.8 0.6 copy-done.8
  63.4 38.6 %shard_map.128 = (bf16[1024,128]{1,0:T(8,128)(2,1)}, bf16[1024,128]{1,0:T(8,128)(2,1)}, bf16[1024,128]{1,0:T(8,128)(2,1)}, bf16[1024,128]{1,0:T(8,128)(2,1)}, f32[40,128]{1,0:T(8,128)}, /*index=5*/f32[512,128]{1,0:T(8,128)}) custom-call(bf16[1024,128]{1,0:T(8,128)(2,1)} %copy-done, bf16[1024,128]{1,0:T(8,128)(2,1)} %copy-done.1, ...), custom_call_target="tpu_custom_call" | custom-call | tf_op jit(solution)/shard_map/pallas_call | solution.py:441
  102.0 0.7 slice_bitcast_fusion
  102.7 0.7 copy.42
  103.4 0.7 copy.41
  104.1 1.0 reshape.59
  105.1 0.1 copy.43
  105.2 0.1 copy.40
  105.3 0.0 copy-start.12
  105.3 0.8 reshape.61
  106.1 0.2 copy-done.12
  106.3 0.0 copy-start.11
  106.3 0.7 copy.48
  107.0 0.3 copy-done.11
  107.3 0.0 copy-start.10
  107.3 0.7 copy.49
  108.0 0.3 copy-done.10
  108.4 0.0 copy-start.9
  108.4 0.7 copy.50
  109.1 0.3 copy-done.9
  109.4 0.7 copy.51
  (5 shorter events, 0.1 us)
Async XLA Ops:
  0.6 0.7 copy-start.14
  0.6 0.8 copy-start.15
  0.7 0.9 copy-start.13
  39.9 1.0 copy-start.4
  40.9 0.9 copy-start.5
  41.8 0.9 copy-start.6
  42.8 0.9 copy-start.7
  60.0 0.7 copy-start
  60.7 0.7 copy-start.1
  61.4 0.7 copy-start.2
  62.1 0.7 copy-start.3
  62.8 0.6 copy-start.8
  105.3 1.0 copy-start.12
  106.3 1.0 copy-start.11
  107.3 1.0 copy-start.10
  108.4 1.0 copy-start.9

commit v3 on v1

v3 whole, which is shorter than its diff:
```python
import functools
import math

import jax
import jax.numpy as jnp
from jax import lax
from jax.experimental import pallas as pl
from jax.experimental.pallas import tpu as pltpu
from jax.sharding import PartitionSpec as P

F32 = jnp.float32
BF16 = jnp.bfloat16
HIGHEST = lax.Precision.HIGHEST
LANES = 128
SUBS = 8
GROUP = 8


def rounded(x):
    return x.astype(BF16).astype(F32)


MESH = pl.DeviceIdType.MESH


def greet(axis, peers, me):
    barrier = pltpu.get_barrier_semaphore()

    def signal(step, carry):
        pl.semaphore_signal(barrier, inc=1, device_id={axis: lax.rem(me + step, peers)}, device_id_type=MESH)
        return carry

    lax.fori_loop(1, peers, signal, 0)
    return barrier


def exchange(own, peers, me, sources, targets, numbers, send_sem, recv_sem):
    def piece(i):
        return pl.ds(pl.multiple_of(i * own, own), own)

    def send(step, carry):
        peer = lax.rem(me + step, peers)
        for n, (source, target) in zip(numbers, zip(sources, targets)):
            pltpu.make_async_remote_copy(
                src_ref=source.at[piece(peer)],
                dst_ref=target.at[piece(me)],
                send_sem=send_sem.at[n],
                recv_sem=recv_sem.at[n],
                device_id={"context": peer},
                device_id_type=MESH,
            ).start()
        return carry

    lax.fori_loop(1, peers, send, 0)


def settle(rows, refs, numbers, sem):
    for n, ref in zip(numbers, refs):
        whole = ref.at[pl.ds(0, rows)]
        pltpu.make_async_copy(whole, whole, sem.at[n]).wait()


def keep(own, me, sources, targets, sem):
    spot = pl.ds(pl.multiple_of(me * own, own), own)
    copies = [
        pltpu.make_async_copy(source.at[spot], target.at[spot], sem.at[n])
        for n, (source, target) in enumerate(zip(sources, targets))
    ]
    for copy in copies:
        copy.start()
    return copies


def operator_kernel(
    own, modes, taps, steps, peers, doubles, used, scale,
    q_ref, k_ref, v_ref, c_ref, taps_ref, residue_ref, rate_ref,
    out_ref, dq_ref, dk_ref, dv_ref, total_ref, shared_ref,
    mq, mk, mv, mc, oo, oq, ok, ov,
    xq, xk, xv, xc, qs, ks, vs, gs, us, ys, ss, aq, ak, av,
    tab, lst, pst, adj, qacc, racc, tacc, small, slots,
    in_send, in_recv, out_send, out_recv, keep_sem, pair_send, pair_recv, tap_send, tap_recv,
):
    me = lax.axis_index("context")
    mine = lax.axis_index("dp")
    barrier = greet("context", peers, me)
    greet("dp", doubles, mine)
    sources, landed = (k_ref, v_ref, q_ref, c_ref), (mk, mv, mq, mc)
    results, outputs = (ok, ov, oo, oq), (dk_ref, dv_ref, out_ref, dq_ref)
    copies = keep(own, me, sources, landed, keep_sem)
    early, late = (0, 1), (2, 3)
    remote = own * (peers - 1)

    lane = lax.broadcasted_iota(jnp.int32, (SUBS, LANES), 1)
    sub = lax.broadcasted_iota(jnp.int32, (SUBS, LANES), 0)
    per_row = LANES // own
    chunk = sub * per_row + lane // own
    chunks = SUBS * per_row

    def later(x, by):
        if by < per_row:
            turned = pltpu.roll(x, own * by, 1)
            x = jnp.where(lane >= own * by, turned, pltpu.roll(turned, 1, 0))
        else:
            x = pltpu.roll(x, by // per_row, 0)
        return jnp.where(chunk >= by, x, 0.0)

    def earlier(x, by):
        if by < per_row:
            turned = pltpu.roll(x, LANES - own * by, 1)
            x = jnp.where(lane < LANES - own * by, turned, pltpu.roll(turned, SUBS - 1, 0))
        else:
            x = pltpu.roll(x, SUBS - by // per_row, 0)
        return jnp.where(chunk < chunks - by, x, 0.0)

    def at(t):
        return pl.ds(pl.multiple_of(t * SUBS, SUBS), SUBS)

    spread = (
        lax.broadcasted_iota(jnp.int32, (own, LANES), 0)
        == lax.broadcasted_iota(jnp.int32, (own, LANES), 1) % own
    ).astype(F32)
    turn = (((0,), (0,)), ((), ()))
    residue = lax.dot_general(residue_ref[...], spread, turn, precision=HIGHEST, preferred_element_type=F32)
    rate = lax.dot_general(rate_ref[...], spread, turn, precision=HIGHEST, preferred_element_type=F32)
    double = 2.0 * rate
    series = 1.0 - double / 7.0
    for n in range(6, 1, -1):
        series = 1.0 - double / float(n) * series
    size = jnp.sqrt(double * series)
    damp = jnp.exp(-rate)
    weighted = residue * size
    chosen = (
        lax.broadcasted_iota(jnp.int32, (LANES, LANES), 0)
        == lax.rem(me, per_row) * own + lax.broadcasted_iota(jnp.int32, (LANES, LANES), 1) % own
    ).astype(F32)
    block = pl.ds(pl.multiple_of(me // per_row * LANES, LANES), LANES)
    n_rows = 2 * modes + 3 * taps
    for m in range(modes):
        tab[pl.ds(m * SUBS, SUBS), :] = jnp.broadcast_to(damp[m : m + 1, :], (SUBS, LANES))
        tab[pl.ds((modes + m) * SUBS, SUBS), :] = jnp.broadcast_to(weighted[m : m + 1, :], (SUBS, LANES))
    far = jnp.exp(rate * (-float(steps)))
    for m in range(modes):
        tab[pl.ds((n_rows + m) * SUBS, SUBS), :] = jnp.broadcast_to(far[m : m + 1, :], (SUBS, LANES))
    for stream in range(3):
        picked = jnp.dot(taps_ref[stream, :, block], chosen, precision=HIGHEST, preferred_element_type=F32)
        for j in range(taps):
            tab[pl.ds((2 * modes + stream * taps + j) * SUBS, SUBS), :] = jnp.broadcast_to(
                picked[j : j + 1, :], (SUBS, LANES)
            )

    def entry(row):
        return tab[pl.ds(row * SUBS, SUBS), :]

    pl.semaphore_wait(barrier, peers + doubles - 2)
    exchange(own, peers, me, sources[:2], landed[:2], early, in_send, in_recv)
    exchange(own, peers, me, sources[2:], landed[2:], late, in_send, in_recv)

    ones = (
        lax.broadcasted_iota(jnp.int32, (LANES, LANES), 0)
        == lax.broadcasted_iota(jnp.int32, (LANES, LANES), 1)
    ).astype(BF16)

    def flipped(x):
        return lax.dot_general(ones, x, (((1,), (1,)), ((), ())), preferred_element_type=F32)

    reach = taps - 1
    head = reach * SUBS
    def unpack(src, dst):
        for i in range(SUBS):
            dst[pl.ds(head + i, steps, stride=SUBS), :] = flipped(src[pl.ds(i * LANES, LANES), :])

    def rim(x):
        for j in range(reach):
            x[pl.ds(j * SUBS, SUBS), :] = later(x[pl.ds(head + (steps - reach + j) * SUBS, SUBS), :], 1)

    def tap(stream, j):
        return entry(2 * modes + stream * taps + j)

    def filtered(x, stream, t):
        total = tap(stream, 0) * x[at(t + reach), :]
        for j in range(1, taps):
            total = total + tap(stream, j) * x[at(t + reach - j), :]
        return rounded(total)

    def pair_features(t, carry):
        key, value = filtered(xk, 1, t), filtered(xv, 2, t)
        ks[at(t), :] = key
        vs[at(t), :] = value
        gs[at(t), :] = rounded(key * value)
        return carry

    def query_features(t, carry):
        query = filtered(xq, 0, t)
        qs[at(t), :] = query
        us[at(t), :] = rounded(xc[at(t + reach), :] * query)
        return carry

    zero = jnp.zeros((SUBS, LANES), F32)
    zeros = tuple(zero for _ in range(modes))

    def ahead_step(t, carry):
        gated = gs[at(t), :]
        return tuple(entry(m) * carry[m] + gated for m in range(modes))

    def back_step(i, carry):
        upstream = us[at(steps - 1 - i), :]
        return tuple(entry(m) * carry[m] + upstream for m in range(modes))

    def chain_ahead(m, carry):
        power, total = tab[at(m + n_rows), :], lst[at(m), :]
        by = 1
        while by < chunks:
            total = total + power * later(total, by)
            power = power * power
            by *= 2
        lst[at(m), :] = later(total, 1)
        return carry

    def chain_back(m, carry):
        power, total = tab[at(m + n_rows), :], pst[at(m), :]
        by = 1
        while by < chunks:
            total = total + power * earlier(total, by)
            power = power * power
            by *= 2
        pst[at(m), :] = earlier(total, 1)
        return carry

    for copy in copies:
        copy.wait()
    settle(remote, landed[:2], early, in_recv)
    unpack(mk, xk)
    unpack(mv, xv)
    rim(xk)
    rim(xv)
    lax.fori_loop(0, steps, pair_features, 0, unroll=4)
    ends = lax.fori_loop(0, steps, ahead_step, zeros, unroll=4)
    for m in range(modes):
        lst[pl.ds(m * SUBS, SUBS), :] = ends[m]
    lax.fori_loop(0, modes, chain_ahead, 0)

    settle(remote, landed[2:], late, in_recv)
    unpack(mq, xq)
    unpack(mc, xc)
    rim(xq)
    lax.fori_loop(0, steps, query_features, 0, unroll=4)
    ends = lax.fori_loop(0, steps, back_step, zeros, unroll=4)
    for m in range(modes):
        pst[pl.ds(m * SUBS, SUBS), :] = ends[m]
    lax.fori_loop(0, modes, chain_back, 0)

    for group in range(0, modes, GROUP):
        members = range(group, group + GROUP)

        def backward(i, carry):
            t = steps - 1 - i
            upstream = us[at(t), :]
            total = zero if group == 0 else ss[at(t), :]
            new = []
            for n, m in enumerate(members):
                state = entry(m) * carry[n] + upstream
                adj[at(t * modes + m), :] = state
                total = total + entry(modes + m) * state
                new.append(state)
            ss[at(t), :] = total
            return tuple(new)

        lax.fori_loop(0, steps, backward, tuple(pst[pl.ds(m * SUBS, SUBS), :] for m in members), unroll=2)

    def closing(a):
        for j in range(reach):
            a[pl.ds((steps + j) * SUBS, SUBS), :] = earlier(a[pl.ds(j * SUBS, SUBS), :], 1)

    def gradient(a, stream, t):
        total = tap(stream, 0) * a[at(t), :]
        for j in range(1, taps):
            total = total + tap(stream, j) * a[at(t + j), :]
        return total

    def pack(src, dst):
        for i in range(SUBS):
            part = src[pl.ds(i, steps, stride=SUBS), :].astype(BF16)
            dst[pl.ds(i * LANES, LANES), :] = flipped(part).astype(BF16)

    def pair_products(t, carry):
        source = rounded(ss[at(t), :])
        new = []
        for n, (other, ref, x) in enumerate(((vs, ak, xk), (ks, av, xv))):
            grad = rounded(source * other[at(t), :])
            ref[at(t), :] = grad
            for j in range(taps):
                new.append(carry[n * taps + j] + grad * x[at(t + reach - j), :])
        return tuple(new)

    def pair_gradients(t, carry):
        ys[at(t), :] = gradient(ak, 1, t)
        ss[at(t), :] = gradient(av, 2, t)
        return carry

    tacc[...] = jnp.zeros(tacc.shape, F32)
    sums = lax.fori_loop(0, steps, pair_products, tuple(zero for _ in range(2 * taps)), unroll=2)
    closing(ak)
    closing(av)
    lax.fori_loop(0, steps, pair_gradients, 0, unroll=4)
    pack(ys, ok)
    pack(ss, ov)
    for n in range(2 * taps):
        tacc[pl.ds(taps + n, 1), :] = jnp.sum(sums[n], axis=0, keepdims=True)
    exchange(own, peers, me, results[:2], outputs[:2], early, out_send, out_recv)
    copies = keep(own, me, results[:2], outputs[:2], keep_sem)

    for group in range(0, modes, GROUP):
        members = range(group, group + GROUP)

        def forward(t, carry):
            states, firsts, seconds = carry
            gated = gs[at(t), :]
            upstream = us[at(t), :]
            total = zero if group == 0 else ys[at(t), :]
            new_s, new_f, new_r = [], [], []
            for n, m in enumerate(members):
                new_r.append(seconds[n] + states[n] * adj[at(t * modes + m), :])
                state = entry(m) * states[n] + gated
                new_f.append(firsts[n] + upstream * state)
                total = total + entry(modes + m) * state
                new_s.append(state)
            ys[at(t), :] = total
            return tuple(new_s), tuple(new_f), tuple(new_r)

        few = tuple(zero for _ in members)
        _, firsts, seconds = lax.fori_loop(
            0, steps, forward, (tuple(lst[pl.ds(m * SUBS, SUBS), :] for m in members), few, few), unroll=2
        )
        for n, m in enumerate(members):
            qacc[pl.ds(m, 1), :] = jnp.sum(firsts[n], axis=0, keepdims=True)
            racc[pl.ds(m, 1), :] = jnp.sum(seconds[n], axis=0, keepdims=True)

    def query_products(t, carry):
        mixed = rounded(ys[at(t), :])
        ys[at(t), :] = qs[at(t), :] * mixed
        grad = rounded(xc[at(t + reach), :] * mixed)
        aq[at(t), :] = grad
        return tuple(carry[j] + grad * xq[at(t + reach - j), :] for j in range(taps))

    def query_gradients(t, carry):
        ss[at(t), :] = gradient(aq, 0, t)
        return carry

    sums = lax.fori_loop(0, steps, query_products, tuple(zero for _ in range(taps)), unroll=2)
    for n in range(taps):
        tacc[pl.ds(n, 1), :] = jnp.sum(sums[n], axis=0, keepdims=True)

    def over_chunks(x):
        by = own
        while by < LANES:
            x = x + pltpu.roll(x, by, 1)
            by *= 2
        return x

    first = over_chunks(qacc[...])
    second = over_chunks(racc[...]) * damp
    small[pl.ds(0, modes), :] = scale * size * first
    bend = residue * (damp * damp / size) * first - weighted * second
    small[pl.ds(modes, modes), :] = scale * rate * bend
    total_taps = scale * over_chunks(tacc[...])
    part = lax.broadcasted_iota(jnp.int32, (1, LANES), 1) // own
    packed = jnp.zeros((SUBS, LANES), F32)
    for n in range(3 * taps):
        spot = (part == n % per_row) & (sub == n // per_row)
        packed = jnp.where(spot, total_taps[n : n + 1, :], packed)
    small[pl.ds(2 * modes, SUBS), :] = packed

    closing(aq)
    lax.fori_loop(0, steps, query_gradients, 0, unroll=4)
    pairs = [
        pltpu.make_async_remote_copy(
            src_ref=small,
            dst_ref=slots.at[mine],
            send_sem=pair_send.at[step],
            recv_sem=pair_recv.at[step],
            device_id={"dp": lax.rem(mine + step, doubles)},
            device_id_type=MESH,
        )
        for step in range(1, doubles)
    ]
    for pair in pairs:
        pair.start()
    own_small = pltpu.make_async_copy(small, slots.at[mine], keep_sem.at[4])
    own_small.start()
    pack(ys, oo)
    pack(ss, oq)
    own_small.wait()
    for pair in pairs:
        pair.wait()
    total = slots[0]
    for n in range(1, doubles):
        total = total + slots[n]
    total_ref[...] = total
    exchange(own, peers, me, results[2:], outputs[2:], late, out_send, out_recv)
    copies += [
        pltpu.make_async_copy(source.at[spot_of(own, me)], target.at[spot_of(own, me)], keep_sem.at[n])
        for n, source, target in zip(late, results[2:], outputs[2:])
    ]
    for copy in copies[2:]:
        copy.start()
    spot = pl.ds(pl.multiple_of(me * SUBS, SUBS), used)
    piece = total_ref.at[pl.ds(2 * modes, used)]

    def send(step, carry):
        pltpu.make_async_remote_copy(
            src_ref=piece,
            dst_ref=shared_ref.at[spot],
            send_sem=tap_send,
            recv_sem=tap_recv,
            device_id={"context": lax.rem(me + step, peers)},
            device_id_type=MESH,
        ).start()
        return carry

    lax.fori_loop(1, peers, send, 0)
    own_taps = pltpu.make_async_copy(piece, shared_ref.at[spot], keep_sem.at[5])
    own_taps.start()
    settle(remote, sources[:2], early, in_send)
    settle(remote, sources[2:], late, in_send)
    for copy in copies:
        copy.wait()
    own_taps.wait()
    for refs, sem in ((outputs, out_recv), (results, out_send)):
        settle(remote, refs, range(4), sem)
    whole = shared_ref.at[pl.ds(0, used * (peers - 1))]
    pltpu.make_async_copy(whole, whole, tap_recv).wait()
    pltpu.make_async_copy(whole, whole, tap_send).wait()


def spot_of(own, me):
    return pl.ds(pl.multiple_of(me * own, own), own)


def closing_kernel(own, modes, taps, *refs):
    sources, total_ref, shared_ref, targets = refs[:4], refs[4], refs[5], refs[6:10]
    taps_ref, residue_ref, rate_ref = refs[10:]
    for source, target in zip(sources, targets):
        target[0] = source[...]
    per_row = LANES // own
    part = lax.broadcasted_iota(jnp.int32, (per_row, LANES), 1) // own
    owner = lax.broadcasted_iota(jnp.int32, (per_row, LANES), 0)
    for b in range(taps_ref.shape[2] // LANES):
        for n in range(3 * taps):
            held = shared_ref[pl.ds(b * per_row * SUBS + n // per_row, per_row, stride=SUBS), :]
            held = jnp.where(part == n % per_row, held, 0.0)
            by = own
            while by < LANES:
                held = held + pltpu.roll(held, by, 1)
                by *= 2
            row = jnp.sum(jnp.where(part == owner, held, 0.0), axis=0, keepdims=True)
            taps_ref[n // taps, pl.ds(n % taps, 1), pl.ds(b * LANES, LANES)] = row
    pick = (
        lax.broadcasted_iota(jnp.int32, (own, LANES), 0) == lax.broadcasted_iota(jnp.int32, (own, LANES), 1)
    ).astype(F32)
    for ref, start in ((residue_ref, 0), (rate_ref, modes)):
        ref[...] = lax.dot_general(
            pick,
            total_ref[pl.ds(start, modes), :],
            (((1,), (1,)), ((), ())),
            precision=HIGHEST,
            preferred_element_type=F32,
        )


def per_device(queries, key_stream, value_stream, cotangent, short_taps, residues, decay_rates):
    channels, steps = queries.shape[1], queries.shape[2]
    own, modes = residues.shape
    taps = short_taps.shape[1]
    owners, doubles = lax.axis_size("context"), lax.axis_size("dp")
    scale = 1.0 / math.sqrt(queries.shape[0] * doubles * steps * owners)
    used = -(-3 * taps * own // LANES)
    wide = jax.ShapeDtypeStruct((channels, steps), BF16)
    small_shape = (2 * modes + SUBS, LANES)
    line, reach = steps * SUBS, taps - 1
    vm = pltpu.VMEM
    here = pl.BlockSpec(memory_space=vm)
    dma = pltpu.SemaphoreType.DMA
    n_rows = 2 * modes + 3 * taps
    tap_rows = -(-3 * taps // SUBS) * SUBS
    shared_shape = jax.ShapeDtypeStruct((owners * SUBS, LANES), F32)
    streams = [x.reshape(channels, steps) for x in (queries, key_stream, value_stream, cotangent)]
    results = pl.pallas_call(
        functools.partial(operator_kernel, own, modes, taps, steps, owners, doubles, used, scale),
        out_shape=[wide] * 4 + [jax.ShapeDtypeStruct(small_shape, F32), shared_shape],
        in_specs=[here] * 7,
        out_specs=[here] * 6,
        scratch_shapes=[vm((channels, steps), BF16)] * 8
        + [vm((line + reach * SUBS, LANES), F32)] * 4
        + [vm((line, LANES), F32)] * 7
        + [vm((line + reach * SUBS, LANES), F32)] * 3
        + [
            vm(((n_rows + modes) * SUBS, LANES), F32),
            vm((modes * SUBS, LANES), F32),
            vm((modes * SUBS, LANES), F32),
            vm((line * modes, LANES), F32),
            vm((modes, LANES), F32),
            vm((modes, LANES), F32),
            vm((tap_rows, LANES), F32),
            vm(small_shape, F32),
            vm((doubles,) + small_shape, F32),
        ]
        + [dma((4,))] * 4
        + [dma((6,)), dma((doubles,)), dma((doubles,)), dma, dma],
        compiler_params=pltpu.CompilerParams(collective_id=0, has_side_effects=True),
    )(*streams, short_taps, residues, decay_rates)
    mode_shape = jax.ShapeDtypeStruct(residues.shape, F32)
    return pl.pallas_call(
        functools.partial(closing_kernel, own, modes, taps),
        out_shape=[jax.ShapeDtypeStruct(queries.shape, BF16)] * 4
        + [jax.ShapeDtypeStruct(short_taps.shape, F32), mode_shape, mode_shape],
        in_specs=[here] * 6,
        out_specs=[here] * 7,
    )(*results)


def solution(mesh):
    stream = P("dp", None, "context")
    in_specs = (stream,) * 4 + (P(), P("context", None), P("context", None))
    out_specs = (stream,) * 4 + (P(), P("context", None), P("context", None))
    return jax.shard_map(per_device, mesh=mesh, in_specs=in_specs, out_specs=out_specs, check_vma=False)
```

time: 199 us -> 85.4 us (0.43)
  the two profiles are of different devices: /device:TPU:32 before, /device:TPU:1 now
where the time goes in v3:
time: 85.4 us; the launch traced here: 85.2 us
  Pallas kernels  84.6 us (99%)
    pallas_call x1, Pallas kernels, per_device(): pl.pallas_call(functools.partial(operator_kernel, own, modes, taps, steps...  82 us
    pallas_call x1, Pallas kernels, per_device(): pl.pallas_call(functools.partial(closing_kernel, own, modes, taps), out_s...  2.61 us

profile of v3, /device:TPU:1, one launch (start us, length us, event | category | flops | bytes accessed | tf_op | source)
XLA Modules:
  0.0 85.2 jit_solution(18201273894477509074)
XLA Ops:
  0.6 82.0 %shard_map.126 = (bf16[1024,128]{1,0:T(8,128)(2,1)}, bf16[1024,128]{1,0:T(8,128)(2,1)}, bf16[1024,128]{1,0:T(8,128)(2,1)}, bf16[1024,128]{1,0:T(8,128)(2,1)}, f32[40,128]{1,0:T(8,128)}, /*index=5*/f32[512,128]{1,0:T(8,128)}) custom-call(bf16[1024,128]{1,0:T(8,128)(2,1)} %bitcast.4, bf16[1024,128]{1,0:T(8,128)(2,1)} %bitcast.5, bf16[1024,128]{1,0:T(8,128)(2,1)} %bitcast.6, ...), custom_call_target="tpu_custom_call" | custom-call | tf_op jit(solution)/shard_map/pallas_call | solution.py:487
  82.6 2.6 %shard_map.127 = (bf16[1,1024,128]{2,1,0:T(8,128)(2,1)}, bf16[1,1024,128]{2,1,0:T(8,128)(2,1)}, bf16[1,1024,128]{2,1,0:T(8,128)(2,1)}, bf16[1,1024,128]{2,1,0:T(...) custom-call(bf16[1024,128]{1,0:T(8,128)(2,1)} %get-tuple-element.13.refs_0_, ...), custom_call_target="tpu_custom_call" | custom-call | tf_op jit(solution)/shard_map/pallas_call | solution.py:512

commit v4 on v1

v4 whole, which is shorter than its diff:
```python
import functools
import math

import jax
import jax.numpy as jnp
from jax import lax
from jax.experimental import pallas as pl
from jax.experimental.pallas import tpu as pltpu
from jax.sharding import PartitionSpec as P

F32 = jnp.float32
BF16 = jnp.bfloat16
HIGHEST = lax.Precision.HIGHEST
LANES = 128
SUBS = 8
GROUP = 8
TALL = 8
WIDE = 4
PLANE = 8


def rounded(x):
    return x.astype(BF16).astype(F32)


MESH = pl.DeviceIdType.MESH


def place(index):
    return index // (TALL * WIDE), lax.rem(index // WIDE, TALL), lax.rem(index, WIDE)


def context_of(y, z, x):
    return (y * TALL + z) * WIDE + x


def settle(ref, send, recv=None):
    pltpu.make_async_copy(ref, ref, send).wait()
    if recv is not None:
        pltpu.make_async_copy(ref, ref, recv).wait()


def operator_kernel(
    modes, taps, steps, doubles, scale,
    q_ref, k_ref, v_ref, c_ref, taps_ref, residue_ref, rate_ref,
    out_ref, dq_ref, dk_ref, dv_ref, shared_ref, dres_ref, drate_ref,
    mq, mk, mv, mc, oo, oq, ok, ov,
    xq, xk, xv, xc, qs, ks, vs, gs, us, ys, ss, aq, ak, av,
    tab, logs, lst, pst, past, qacc, racc, tacc,
    tsrc, tin, fsrc, fin, bsrc, bin_, rims, tails, small, stack, slots, total_ref,
    in_send, in_recv, out_send, out_recv, keep_sem, pair_send, pair_recv,
    rim_send, rim_recv, tail_send, tail_recv, line_send, line_recv, tap_send, tap_recv,
):
    y, z, x = place(lax.axis_index("context"))
    mine = lax.axis_index("dp")
    spot = y * WIDE + x
    own = residue_ref.shape[0]
    barrier = pltpu.get_barrier_semaphore()

    def across(step):
        s = lax.rem(spot + step, PLANE)
        return s, {"context": context_of(s // WIDE, z, lax.rem(s, WIDE))}

    def along(step):
        return {"context": context_of(y, lax.rem(z + step, TALL), x)}

    for step in range(1, PLANE):
        pl.semaphore_signal(barrier, inc=1, device_id=across(step)[1], device_id_type=MESH)
    for step in range(1, TALL):
        pl.semaphore_signal(barrier, inc=1, device_id=along(step), device_id_type=MESH)
    for step in range(1, doubles):
        pl.semaphore_signal(
            barrier, inc=1, device_id={"dp": lax.rem(mine + step, doubles)}, device_id_type=MESH
        )

    sources, landed = (k_ref, v_ref, q_ref, c_ref), (mk, mv, mq, mc)
    kept = [
        pltpu.make_async_copy(sources[n].at[y, :, x], landed[n].at[spot], keep_sem.at[n]) for n in range(4)
    ]
    for copy in kept:
        copy.start()

    lane = lax.broadcasted_iota(jnp.int32, (SUBS, LANES), 1)
    sub = lax.broadcasted_iota(jnp.int32, (SUBS, LANES), 0)
    step_x = lax.rem(sub, WIDE)
    high = sub >= WIDE

    def at(t):
        return pl.ds(pl.multiple_of(t * SUBS, SUBS), SUBS)

    def fixed(row):
        return pl.ds(row * SUBS, SUBS)

    mine_lanes = (
        lax.broadcasted_iota(jnp.int32, (own, LANES), 1)
        == z * own + lax.broadcasted_iota(jnp.int32, (own, LANES), 0)
    ).astype(F32)
    turn = (((0,), (0,)), ((), ()))
    tsrc[pl.ds(0, modes), :] = lax.dot_general(
        residue_ref[...], mine_lanes, turn, precision=HIGHEST, preferred_element_type=F32
    )
    tsrc[pl.ds(modes, modes), :] = lax.dot_general(
        rate_ref[...], mine_lanes, turn, precision=HIGHEST, preferred_element_type=F32
    )
    half = taps_ref.shape[2] // 2
    column = lax.broadcasted_iota(jnp.int32, (half, LANES), 1)
    chosen = (
        lax.broadcasted_iota(jnp.int32, (half, LANES), 0)
        == column // own * (WIDE * own) + x * own + lax.rem(column, own)
    ).astype(F32)
    block = pl.ds(pl.multiple_of(y * half, half), half)
    n_taps = 2 * modes
    for stream in range(3):
        picked = jnp.dot(taps_ref[stream, :, block], chosen, precision=HIGHEST, preferred_element_type=F32)
        for j in range(taps):
            tab[fixed(n_taps + stream * taps + j), :] = jnp.broadcast_to(picked[j : j + 1, :], (SUBS, LANES))
    tacc[...] = jnp.zeros(tacc.shape, F32)

    def line(src, dst, n):
        for step in range(1, TALL):
            pltpu.make_async_remote_copy(
                src_ref=src,
                dst_ref=dst.at[z],
                send_sem=line_send.at[n],
                recv_sem=line_recv.at[n],
                device_id=along(step),
                device_id_type=MESH,
            ).start()
        copy = pltpu.make_async_copy(src, dst.at[z], keep_sem.at[8 + n])
        copy.start()
        return copy

    def line_wait(copy, dst, n):
        copy.wait()
        settle(dst.at[pl.ds(0, TALL - 1)], line_send.at[n], line_recv.at[n])

    pl.semaphore_wait(barrier, PLANE + TALL + doubles - 3)
    table_copy = line(tsrc, tin, 0)
    for n in range(4):
        for step in range(1, PLANE):
            s, peer = across(step)
            pltpu.make_async_remote_copy(
                src_ref=sources[n].at[s // WIDE, :, lax.rem(s, WIDE)],
                dst_ref=landed[n].at[spot],
                send_sem=in_send.at[n],
                recv_sem=in_recv.at[n],
                device_id=peer,
                device_id_type=MESH,
            ).start()

    line_wait(table_copy, tin, 0)
    tables = tin[0]
    for n in range(1, TALL):
        tables = tables + tin[n]
    residue, rate = tables[:modes], tables[modes:]
    double = 2.0 * rate
    series = 1.0 - double / 7.0
    for n in range(6, 1, -1):
        series = 1.0 - double / float(n) * series
    size = jnp.sqrt(double * series)
    damp = jnp.exp(-rate)
    weighted = residue * size
    for m in range(modes):
        tab[fixed(m), :] = jnp.broadcast_to(damp[m : m + 1, :], (SUBS, LANES))
        tab[fixed(modes + m), :] = jnp.broadcast_to(weighted[m : m + 1, :], (SUBS, LANES))
        logs[fixed(m), :] = jnp.broadcast_to(-float(steps) * rate[m : m + 1, :], (SUBS, LANES))

    def entry(row):
        return tab[fixed(row), :]

    ones = (
        lax.broadcasted_iota(jnp.int32, (LANES, LANES), 0)
        == lax.broadcasted_iota(jnp.int32, (LANES, LANES), 1)
    ).astype(BF16)

    def flipped(value):
        return lax.dot_general(ones, value, (((1,), (1,)), ((), ())), preferred_element_type=F32)

    reach = taps - 1
    head = reach * SUBS

    def unpack(n, dst):
        kept[n].wait()
        settle(landed[n].at[pl.ds(0, PLANE - 1)], in_recv.at[n])
        for i in range(PLANE):
            dst[pl.ds(head + i, steps, stride=SUBS), :] = flipped(landed[n][i].reshape(LANES, steps))

    def rim_copy(n, src):
        return pltpu.make_async_remote_copy(
            src_ref=src.at[pl.ds(steps * SUBS, head)],
            dst_ref=rims.at[n],
            send_sem=rim_send.at[n],
            recv_sem=rim_recv.at[n],
            device_id=along(1),
            device_id_type=MESH,
        )

    def tail_copy(n, src):
        return pltpu.make_async_remote_copy(
            src_ref=src.at[pl.ds(0, head)],
            dst_ref=tails.at[n],
            send_sem=tail_send.at[n],
            recv_sem=tail_recv.at[n],
            device_id=along(TALL - 1),
            device_id_type=MESH,
        )

    first_z, last_z = z == 0, z == TALL - 1

    def before(value, outer):
        lowest = jnp.where(high, pltpu.roll(outer, 1, 0), 0.0)
        outer = jnp.where(first_z, lowest, pltpu.roll(outer, 5, 0))
        return jnp.where(step_x > 0, pltpu.roll(value, 1, 0), outer)

    def after(value, outer):
        highest = jnp.where(high, 0.0, pltpu.roll(outer, 7, 0))
        outer = jnp.where(last_z, highest, pltpu.roll(outer, 3, 0))
        return jnp.where(step_x < WIDE - 1, pltpu.roll(value, 7, 0), outer)

    def rim(n, ref):
        for j in range(reach):
            ref[fixed(j), :] = before(ref[fixed(steps + j), :], rims[n, fixed(j), :])

    def tail(n, ref):
        for j in range(reach):
            ref[fixed(steps + j), :] = after(ref[fixed(j), :], tails[n, fixed(j), :])

    def tap(stream, j):
        return entry(n_taps + stream * taps + j)

    def filtered(ref, stream, t):
        total = tap(stream, 0) * ref[at(t + reach), :]
        for j in range(1, taps):
            total = total + tap(stream, j) * ref[at(t + reach - j), :]
        return rounded(total)

    def pair_features(t, carry):
        key, value = filtered(xk, 1, t), filtered(xv, 2, t)
        ks[at(t), :] = key
        vs[at(t), :] = value
        gs[at(t), :] = rounded(key * value)
        return carry

    def query_features(t, carry):
        query = filtered(xq, 0, t)
        qs[at(t), :] = query
        us[at(t), :] = rounded(xc[at(t + reach), :] * query)
        return carry

    zero = jnp.zeros((SUBS, LANES), F32)
    zeros = tuple(zero for _ in range(modes))

    def ahead_step(t, carry):
        gated = gs[at(t), :]
        return tuple(entry(m) * carry[m] + gated for m in range(modes))

    def back_step(i, carry):
        upstream = us[at(steps - 1 - i), :]
        return tuple(entry(m) * carry[m] + upstream for m in range(modes))

    def scan_ahead(value, m):
        power = jnp.exp(logs[fixed(m), :])
        for by in (1, 2):
            value = value + power * jnp.where(step_x >= by, pltpu.roll(value, by, 0), 0.0)
            power = power * power
        return value

    def scan_back(value, m):
        power = jnp.exp(logs[fixed(m), :])
        for by in (1, 2):
            value = value + power * jnp.where(step_x < WIDE - by, pltpu.roll(value, SUBS - by, 0), 0.0)
            power = power * power
        return value

    def ahead_row(n):
        return step_x == WIDE - 1 - n

    def back_row(n):
        return step_x == n

    def finish_ends(ends, scan, store, src, row_of, sign):
        for g in range(modes // WIDE):
            packed = zero
            for n in range(WIDE):
                m = g * WIDE + n
                value = scan(ends[m], m)
                store[fixed(m), :] = value
                packed = jnp.where(row_of(n), value if n == 0 else pltpu.roll(value, (sign * n) % SUBS, 0), packed)
            src[fixed(g), :] = packed

    def seeds(store, held, row_of, sign, order, inside, leap, fresh, weight):
        for g in range(modes // WIDE):
            slow = zero
            for n in range(WIDE):
                slow = jnp.where(row_of(n), logs[fixed(g * WIDE + n), :], slow)
            far = jnp.exp(float(WIDE) * slow)
            full, part = zero, zero
            for other in order:
                value = held[other, fixed(g), :]
                full = far * full + value
                part = jnp.where(inside(other), far * part + value, part)
            part = part + jnp.where(fresh, jnp.exp(slow * leap) * pltpu.roll(full, WIDE, 0), 0.0)
            for n in range(WIDE):
                m = g * WIDE + n
                value = jnp.where(row_of(n), part, 0.0)
                if n:
                    value = pltpu.roll(value, (-sign * n) % SUBS, 0)
                value = value + pltpu.roll(value, sign % SUBS, 0)
                value = value + pltpu.roll(value, (2 * sign) % SUBS, 0)
                value = jnp.exp(logs[fixed(m), :] * weight) * value
                near = pltpu.roll(store[fixed(m), :], (-sign) % SUBS, 0)
                keep = step_x > 0 if sign < 0 else step_x < WIDE - 1
                store[fixed(m), :] = jnp.where(keep, near, 0.0) + value

    float_x = step_x.astype(F32)
    float_z = z.astype(F32)

    unpack(0, xk)
    unpack(1, xv)
    rim_copies = [rim_copy(0, xk), rim_copy(1, xv)]
    for copy in rim_copies:
        copy.start()
    unpack(2, xq)
    for copy in rim_copies:
        copy.wait()
    rim(0, xk)
    rim(1, xv)
    rim_copies = [rim_copy(2, xq)]
    rim_copies[0].start()
    lax.fori_loop(0, steps, pair_features, 0, unroll=4)
    ends = lax.fori_loop(0, steps, ahead_step, zeros, unroll=4)
    finish_ends(ends, scan_ahead, lst, fsrc, ahead_row, -1)
    rim_copies[0].wait()
    rim(2, xq)
    ahead_copy = line(fsrc, fin, 1)

    unpack(3, xc)
    lax.fori_loop(0, steps, query_features, 0, unroll=4)
    ends = lax.fori_loop(0, steps, back_step, zeros, unroll=4)
    finish_ends(ends, scan_back, pst, bsrc, back_row, 1)
    line_wait(ahead_copy, fin, 1)
    back_copy = line(bsrc, bin_, 2)
    seeds(
        lst, fin, ahead_row, -1, range(TALL), lambda other: other < z, float(WIDE) * float_z, high, float_x
    )

    for group in range(0, modes, GROUP):
        members = range(group, group + GROUP)

        def forward(t, carry):
            states, firsts = carry
            gated = gs[at(t), :]
            upstream = us[at(t), :]
            total = zero if group == 0 else ys[at(t), :]
            new_s, new_f = [], []
            for n, m in enumerate(members):
                past[at(t * modes + m), :] = states[n]
                state = entry(m) * states[n] + gated
                new_f.append(firsts[n] + upstream * state)
                total = total + entry(modes + m) * state
                new_s.append(state)
            ys[at(t), :] = total
            return tuple(new_s), tuple(new_f)

        few = tuple(zero for _ in members)
        _, firsts = lax.fori_loop(0, steps, forward, (tuple(lst[fixed(m), :] for m in members), few), unroll=2)
        for n, m in enumerate(members):
            qacc[pl.ds(m, 1), :] = jnp.sum(firsts[n], axis=0, keepdims=True)

    def gradient(a, stream, t):
        total = tap(stream, 0) * a[at(t), :]
        for j in range(1, taps):
            total = total + tap(stream, j) * a[at(t + j), :]
        return total

    def pack(src, dst):
        for i in range(PLANE):
            value = src[pl.ds(i, steps, stride=SUBS), :].astype(BF16)
            dst[i] = flipped(value).astype(BF16).reshape(dst.shape[1:])

    def query_products(t, carry):
        mixed = rounded(ys[at(t), :])
        ys[at(t), :] = qs[at(t), :] * mixed
        grad = rounded(xc[at(t + reach), :] * mixed)
        aq[at(t), :] = grad
        return tuple(carry[j] + grad * xq[at(t + reach - j), :] for j in range(taps))

    def query_gradients(t, carry):
        ss[at(t), :] = gradient(aq, 0, t)
        return carry

    results, outputs = (oo, oq, ok, ov), (out_ref, dq_ref, dk_ref, dv_ref)
    kept_out = []

    def deliver(n):
        for step in range(1, PLANE):
            s, peer = across(step)
            pltpu.make_async_remote_copy(
                src_ref=results[n].at[s],
                dst_ref=outputs[n].at[y, :, x],
                send_sem=out_send.at[n],
                recv_sem=out_recv.at[n],
                device_id=peer,
                device_id_type=MESH,
            ).start()
        copy = pltpu.make_async_copy(results[n].at[spot], outputs[n].at[y, :, x], keep_sem.at[4 + n])
        copy.start()
        kept_out.append(copy)

    sums = lax.fori_loop(0, steps, query_products, tuple(zero for _ in range(taps)), unroll=2)
    for n in range(taps):
        tacc[pl.ds(n, 1), :] = jnp.sum(sums[n], axis=0, keepdims=True)
    query_tail = tail_copy(0, aq)
    query_tail.start()
    pack(ys, oo)
    line_wait(back_copy, bin_, 2)
    deliver(0)
    seeds(
        pst, bin_, back_row, 1, range(TALL - 1, -1, -1), lambda other: other > z,
        float(WIDE) * (float(TALL - 1) - float_z), jnp.logical_not(high), float(WIDE - 1) - float_x,
    )
    query_tail.wait()
    tail(0, aq)
    lax.fori_loop(0, steps, query_gradients, 0, unroll=4)
    pack(ss, oq)

    for group in range(0, modes, GROUP):
        members = range(group, group + GROUP)

        def backward(i, carry):
            states, seconds = carry
            t = steps - 1 - i
            upstream = us[at(t), :]
            total = zero if group == 0 else ss[at(t), :]
            new_s, new_r = [], []
            for n, m in enumerate(members):
                state = entry(m) * states[n] + upstream
                new_r.append(seconds[n] + state * past[at(t * modes + m), :])
                total = total + entry(modes + m) * state
                new_s.append(state)
            ss[at(t), :] = total
            return tuple(new_s), tuple(new_r)

        few = tuple(zero for _ in members)
        _, seconds = lax.fori_loop(0, steps, backward, (tuple(pst[fixed(m), :] for m in members), few), unroll=2)
        for n, m in enumerate(members):
            racc[pl.ds(m, 1), :] = jnp.sum(seconds[n], axis=0, keepdims=True)
        if group == 0:
            deliver(1)

    def pair_products(t, carry):
        source = rounded(ss[at(t), :])
        new = []
        for n, (other, ref, x_ref) in enumerate(((vs, ak, xk), (ks, av, xv))):
            grad = rounded(source * other[at(t), :])
            ref[at(t), :] = grad
            for j in range(taps):
                new.append(carry[n * taps + j] + grad * x_ref[at(t + reach - j), :])
        return tuple(new)

    def pair_gradients(t, carry):
        ys[at(t), :] = gradient(ak, 1, t)
        ss[at(t), :] = gradient(av, 2, t)
        return carry

    sums = lax.fori_loop(0, steps, pair_products, tuple(zero for _ in range(2 * taps)), unroll=2)
    for n in range(2 * taps):
        tacc[pl.ds(taps + n, 1), :] = jnp.sum(sums[n], axis=0, keepdims=True)
    tail_copies = [tail_copy(1, ak), tail_copy(2, av)]
    for copy in tail_copies:
        copy.start()
    first, second = qacc[...], racc[...] * damp
    small[pl.ds(0, modes), :] = scale * size * first
    small[pl.ds(modes, modes), :] = scale * rate * (residue * (damp * damp / size) * first - weighted * second)
    small[pl.ds(2 * modes, tacc.shape[0]), :] = scale * tacc[...]
    for copy in tail_copies:
        copy.wait()
    small_copy = line(small, stack, 3)
    tail(1, ak)
    tail(2, av)
    lax.fori_loop(0, steps, pair_gradients, 0, unroll=4)
    pack(ys, ok)
    pack(ss, ov)

    line_wait(small_copy, stack, 3)
    total = stack[0]
    for n in range(1, TALL):
        total = total + stack[n]
    slots[doubles] = total
    deliver(2)
    deliver(3)
    pairs = [
        pltpu.make_async_remote_copy(
            src_ref=slots.at[doubles],
            dst_ref=slots.at[mine],
            send_sem=pair_send.at[step],
            recv_sem=pair_recv.at[step],
            device_id={"dp": lax.rem(mine + step, doubles)},
            device_id_type=MESH,
        )
        for step in range(1, doubles)
    ]
    for pair in pairs:
        pair.start()
    own_small = pltpu.make_async_copy(slots.at[doubles], slots.at[mine], keep_sem.at[12])
    own_small.start()
    own_small.wait()
    for pair in pairs:
        pair.wait()
    total = slots[0]
    for n in range(1, doubles):
        total = total + slots[n]
    total_ref[...] = total[2 * modes :]
    for ref, start in ((dres_ref, 0), (drate_ref, modes)):
        ref[...] = lax.dot_general(
            mine_lanes,
            total[start : start + modes],
            (((1,), (1,)), ((), ())),
            precision=HIGHEST,
            preferred_element_type=F32,
        )
    for step in range(1, PLANE):
        pltpu.make_async_remote_copy(
            src_ref=total_ref,
            dst_ref=shared_ref.at[spot],
            send_sem=tap_send,
            recv_sem=tap_recv,
            device_id=across(step)[1],
            device_id_type=MESH,
        ).start()
    own_taps = pltpu.make_async_copy(total_ref, shared_ref.at[spot], keep_sem.at[13])
    own_taps.start()
    for n in range(4):
        settle(landed[n].at[pl.ds(0, PLANE - 1)], in_send.at[n])
    for copy in kept_out:
        copy.wait()
    own_taps.wait()
    for n in range(4):
        settle(results[n].at[pl.ds(0, PLANE - 1)], out_send.at[n])
        settle(outputs[n].at[:, pl.ds(0, TALL - 1)], out_recv.at[n])
    settle(shared_ref.at[pl.ds(0, PLANE - 1)], tap_send, tap_recv)


def closing_kernel(own, taps, *refs):
    sources, shared_ref, parts, targets = refs[:4], refs[4], refs[5:7], refs[7:11]
    taps_ref, finals = refs[11], refs[12:]
    for source, target in zip(sources, targets):
        target[0] = source[...].reshape(target.shape[1:])
    for part, final in zip(parts, finals):
        final[...] = part[...]
    rows = shared_ref.shape[1]
    group = lax.broadcasted_iota(jnp.int32, (rows, LANES), 1) // own
    groups = LANES // own
    for b in range(taps_ref.shape[2] // LANES):
        y, pair = b // WIDE, b % WIDE
        value = jnp.zeros((rows, LANES), F32)
        for spot in range(groups):
            z, x = pair * (groups // WIDE) + spot // WIDE, spot % WIDE
            held = shared_ref[y * WIDE + x]
            held = pltpu.roll(held, (spot - z) * own % LANES, 1)
            value = jnp.where(group == spot, held, value)
        for stream in range(3):
            taps_ref[stream, :, pl.ds(b * LANES, LANES)] = value[stream * taps : (stream + 1) * taps]


def per_device(queries, key_stream, value_stream, cotangent, short_taps, residues, decay_rates):
    channels, steps = queries.shape[1], queries.shape[2]
    own, modes = residues.shape
    taps = short_taps.shape[1]
    owners, doubles = lax.axis_size("context"), lax.axis_size("dp")
    scale = 1.0 / math.sqrt(queries.shape[0] * doubles * steps * owners)
    view = (owners // (TALL * WIDE), TALL, WIDE, own, steps)
    wide = jax.ShapeDtypeStruct(view, BF16)
    mode_shape = jax.ShapeDtypeStruct(residues.shape, F32)
    line, reach = steps * SUBS, taps - 1
    vm = pltpu.VMEM
    here = pl.BlockSpec(memory_space=vm)
    dma = pltpu.SemaphoreType.DMA
    tap_rows = -(-3 * taps // SUBS) * SUBS
    rows = 2 * modes + tap_rows
    ends = modes // WIDE * SUBS
    streams = [x.reshape(view) for x in (queries, key_stream, value_stream, cotangent)]
    results = pl.pallas_call(
        functools.partial(operator_kernel, modes, taps, steps, doubles, scale),
        out_shape=[wide] * 4 + [jax.ShapeDtypeStruct((PLANE, tap_rows, LANES), F32), mode_shape, mode_shape],
        in_specs=[here] * 7,
        out_specs=[here] * 7,
        scratch_shapes=[vm((PLANE, TALL, own, steps), BF16)] * 8
        + [vm((line + reach * SUBS, LANES), F32)] * 4
        + [vm((line, LANES), F32)] * 7
        + [vm((line + reach * SUBS, LANES), F32)] * 3
        + [
            vm(((2 * modes + 3 * taps) * SUBS, LANES), F32),
            vm((modes * SUBS, LANES), F32),
            vm((modes * SUBS, LANES), F32),
            vm((modes * SUBS, LANES), F32),
            vm((line * modes, LANES), F32),
            vm((modes, LANES), F32),
            vm((modes, LANES), F32),
            vm((tap_rows, LANES), F32),
            vm((2 * modes, LANES), F32),
            vm((TALL, 2 * modes, LANES), F32),
            vm((ends, LANES), F32),
            vm((TALL, ends, LANES), F32),
            vm((ends, LANES), F32),
            vm((TALL, ends, LANES), F32),
            vm((3, reach * SUBS, LANES), F32),
            vm((3, reach * SUBS, LANES), F32),
            vm((rows, LANES), F32),
            vm((TALL, rows, LANES), F32),
            vm((doubles + 1, rows, LANES), F32),
            vm((tap_rows, LANES), F32),
        ]
        + [dma((4,))] * 4
        + [dma((14,)), dma((doubles,)), dma((doubles,))]
        + [dma((3,))] * 4
        + [dma((4,))] * 2
        + [dma, dma],
        compiler_params=pltpu.CompilerParams(collective_id=0, has_side_effects=True),
    )(*streams, short_taps, residues, decay_rates)
    return pl.pallas_call(
        functools.partial(closing_kernel, own, taps),
        out_shape=[jax.ShapeDtypeStruct(queries.shape, BF16)] * 4
        + [jax.ShapeDtypeStruct(short_taps.shape, F32), mode_shape, mode_shape],
        in_specs=[here] * 7,
        out_specs=[here] * 7,
    )(*results)


def solution(mesh):
    stream = P("dp", None, "context")
    in_specs = (stream,) * 4 + (P(), P("context", None), P("context", None))
    out_specs = (stream,) * 4 + (P(), P("context", None), P("context", None))
    return jax.shard_map(per_device, mesh=mesh, in_specs=in_specs, out_specs=out_specs, check_vma=False)
```

time: 199 us -> 68.5 us (0.34)
  the two profiles are of different devices: /device:TPU:32 before, /device:TPU:1 now
where the time goes in v4:
time: 68.5 us; the launch traced here: 68.4 us
  Pallas kernels  67.8 us (99%)
    pallas_call x1, Pallas kernels, per_device(): pl.pallas_call(functools.partial(operator_kernel, modes, taps, steps, dou...  65.4 us
    pallas_call x1, Pallas kernels, per_device(): pl.pallas_call(functools.partial(closing_kernel, own, taps), out_shape=[j...  2.31 us

profile of v4, /device:TPU:1, one launch (start us, length us, event | category | flops | bytes accessed | tf_op | source)
XLA Modules:
  0.0 68.4 jit_solution(7671603254992583571)
XLA Ops:
  0.6 65.4 %shard_map.126 = (bf16[2,8,4,16,128]{4,3,2,1,0:T(8,128)(2,1)}, bf16[2,8,4,16,128]{4,3,2,1,0:T(8,128)(2,1)}, bf16[2,8,4,16,128]{4,3,2,1,0:T(8,128)(2,1)}, bf16[2,...) custom-call(bf16[2,8,4,16,128]{4,3,2,1,0:T(8,128)(2,1)} %bitcast.4, ...), custom_call_target="tpu_custom_call" | custom-call | tf_op jit(solution)/shard_map/pallas_call | solution.py:583
  66.1 2.3 %shard_map.127 = (bf16[1,1024,128]{2,1,0:T(8,128)(2,1)}, bf16[1,1024,128]{2,1,0:T(8,128)(2,1)}, bf16[1,1024,128]{2,1,0:T(8,128)(2,1)}, bf16[1,1024,128]{2,1,0:T(...) custom-call(bf16[2,8,4,16,128]{4,3,2,1,0:T(8,128)(2,1)} %get-tuple-element.14.refs_0_, ...), custom_call_target="tpu_custom_call" | custom-call | tf_op jit(solution)/shard_map/pallas_call | solution.py:621

commit v5 on v4

--- a/solution.py
+++ b/solution.py
@@ -47,7 +47,8 @@
     mq, mk, mv, mc, oo, oq, ok, ov,
     xq, xk, xv, xc, qs, ks, vs, gs, us, ys, ss, aq, ak, av,
     tab, logs, lst, pst, past, qacc, racc, tacc,
-    tsrc, tin, fsrc, fin, bsrc, bin_, rims, tails, small, stack, slots, total_ref,
+    tsrc, tin, fsrc, fin, bsrc, bin_, rims, tails,
+    tap_part, tap_stack, tap_slots, mode_part, mode_stack, mode_slots, total_ref,
     in_send, in_recv, out_send, out_recv, keep_sem, pair_send, pair_recv,
     rim_send, rim_recv, tail_send, tail_recv, line_send, line_recv, tap_send, tap_recv,
 ):
@@ -320,26 +321,31 @@
     rim_copies = [rim_copy(0, xk), rim_copy(1, xv)]
     for copy in rim_copies:
         copy.start()
-    unpack(2, xq)
+    lax.fori_loop(reach, steps, pair_features, 0, unroll=6)
+    ends = lax.fori_loop(reach, steps, ahead_step, zeros, unroll=6)
     for copy in rim_copies:
         copy.wait()
     rim(0, xk)
     rim(1, xv)
-    rim_copies = [rim_copy(2, xq)]
-    rim_copies[0].start()
-    lax.fori_loop(0, steps, pair_features, 0, unroll=4)
-    ends = lax.fori_loop(0, steps, ahead_step, zeros, unroll=4)
+    for t in range(reach):
+        pair_features(t, 0)
+    ends = list(ends)
+    for m in range(modes):
+        for t in range(reach):
+            ends[m] = ends[m] + jnp.exp(logs[fixed(m), :] * (float(steps - 1 - t) / steps)) * gs[fixed(t), :]
     finish_ends(ends, scan_ahead, lst, fsrc, ahead_row, -1)
-    rim_copies[0].wait()
+    unpack(2, xq)
+    ahead_copy = line(fsrc, fin, 1)
+    query_rim = rim_copy(2, xq)
+    query_rim.start()
+    unpack(3, xc)
+    query_rim.wait()
     rim(2, xq)
-    ahead_copy = line(fsrc, fin, 1)
-
-    unpack(3, xc)
     lax.fori_loop(0, steps, query_features, 0, unroll=4)
     ends = lax.fori_loop(0, steps, back_step, zeros, unroll=4)
     finish_ends(ends, scan_back, pst, bsrc, back_row, 1)
+    back_copy = line(bsrc, bin_, 2)
     line_wait(ahead_copy, fin, 1)
-    back_copy = line(bsrc, bin_, 2)
     seeds(
         lst, fin, ahead_row, -1, range(TALL), lambda other: other < z, float(WIDE) * float_z, high, float_x
     )
@@ -413,16 +419,17 @@
     query_tail = tail_copy(0, aq)
     query_tail.start()
     pack(ys, oo)
+    query_tail.wait()
+    tail(0, aq)
+    deliver(0)
+    lax.fori_loop(0, steps, query_gradients, 0, unroll=4)
+    pack(ss, oq)
     line_wait(back_copy, bin_, 2)
-    deliver(0)
     seeds(
         pst, bin_, back_row, 1, range(TALL - 1, -1, -1), lambda other: other > z,
         float(WIDE) * (float(TALL - 1) - float_z), jnp.logical_not(high), float(WIDE - 1) - float_x,
     )
-    query_tail.wait()
-    tail(0, aq)
-    lax.fori_loop(0, steps, query_gradients, 0, unroll=4)
-    pack(ss, oq)
+    deliver(1)
 
     for group in range(0, modes, GROUP):
         members = range(group, group + GROUP)
@@ -445,8 +452,6 @@
         _, seconds = lax.fori_loop(0, steps, backward, (tuple(pst[fixed(m), :] for m in members), few), unroll=2)
         for n, m in enumerate(members):
             racc[pl.ds(m, 1), :] = jnp.sum(seconds[n], axis=0, keepdims=True)
-        if group == 0:
-            deliver(1)
 
     def pair_products(t, carry):
         source = rounded(ss[at(t), :])
@@ -469,56 +474,58 @@
     tail_copies = [tail_copy(1, ak), tail_copy(2, av)]
     for copy in tail_copies:
         copy.start()
+    tap_part[...] = scale * tacc[...]
     first, second = qacc[...], racc[...] * damp
-    small[pl.ds(0, modes), :] = scale * size * first
-    small[pl.ds(modes, modes), :] = scale * rate * (residue * (damp * damp / size) * first - weighted * second)
-    small[pl.ds(2 * modes, tacc.shape[0]), :] = scale * tacc[...]
+    mode_part[pl.ds(0, modes), :] = scale * size * first
+    mode_part[pl.ds(modes, modes), :] = (
+        scale * rate * (residue * (damp * damp / size) * first - weighted * second)
+    )
+    tap_copy = line(tap_part, tap_stack, 3)
+    mode_copy = line(mode_part, mode_stack, 4)
+    lax.fori_loop(0, steps - reach, pair_gradients, 0, unroll=6)
     for copy in tail_copies:
         copy.wait()
-    small_copy = line(small, stack, 3)
     tail(1, ak)
     tail(2, av)
-    lax.fori_loop(0, steps, pair_gradients, 0, unroll=4)
+    for t in range(steps - reach, steps):
+        pair_gradients(t, 0)
     pack(ys, ok)
     pack(ss, ov)
-
-    line_wait(small_copy, stack, 3)
-    total = stack[0]
-    for n in range(1, TALL):
-        total = total + stack[n]
-    slots[doubles] = total
     deliver(2)
     deliver(3)
-    pairs = [
-        pltpu.make_async_remote_copy(
-            src_ref=slots.at[doubles],
-            dst_ref=slots.at[mine],
-            send_sem=pair_send.at[step],
-            recv_sem=pair_recv.at[step],
-            device_id={"dp": lax.rem(mine + step, doubles)},
-            device_id_type=MESH,
-        )
-        for step in range(1, doubles)
-    ]
-    for pair in pairs:
-        pair.start()
-    own_small = pltpu.make_async_copy(slots.at[doubles], slots.at[mine], keep_sem.at[12])
-    own_small.start()
-    own_small.wait()
-    for pair in pairs:
+
+    def summed(ref, count):
+        total = ref[0]
+        for n in range(1, count):
+            total = total + ref[n]
+        return total
+
+    def pairs_of(ref, base):
+        local = pltpu.make_async_copy(ref.at[doubles], ref.at[mine], keep_sem.at[13 + base])
+        copies = [
+            pltpu.make_async_remote_copy(
+                src_ref=ref.at[doubles],
+                dst_ref=ref.at[mine],
+                send_sem=pair_send.at[base * doubles + step],
+                recv_sem=pair_recv.at[base * doubles + step],
+                device_id={"dp": lax.rem(mine + step, doubles)},
+                device_id_type=MESH,
+            )
+            for step in range(1, doubles)
+        ]
+        for copy in copies + [local]:
+            copy.start()
+        return copies + [local]
+
+    line_wait(tap_copy, tap_stack, 3)
+    tap_slots[doubles] = summed(tap_stack, TALL)
+    tap_pairs = pairs_of(tap_slots, 0)
+    line_wait(mode_copy, mode_stack, 4)
+    mode_slots[doubles] = summed(mode_stack, TALL)
+    for pair in tap_pairs:
         pair.wait()
-    total = slots[0]
-    for n in range(1, doubles):
-        total = total + slots[n]
-    total_ref[...] = total[2 * modes :]
-    for ref, start in ((dres_ref, 0), (drate_ref, modes)):
-        ref[...] = lax.dot_general(
-            mine_lanes,
-            total[start : start + modes],
-            (((1,), (1,)), ((), ())),
-            precision=HIGHEST,
-            preferred_element_type=F32,
-        )
+    total_ref[...] = summed(tap_slots, doubles)
+    mode_pairs = pairs_of(mode_slots, 1)
     for step in range(1, PLANE):
         pltpu.make_async_remote_copy(
             src_ref=total_ref,
@@ -528,8 +535,19 @@
             device_id=across(step)[1],
             device_id_type=MESH,
         ).start()
-    own_taps = pltpu.make_async_copy(total_ref, shared_ref.at[spot], keep_sem.at[13])
+    own_taps = pltpu.make_async_copy(total_ref, shared_ref.at[spot], keep_sem.at[15])
     own_taps.start()
+    for pair in mode_pairs:
+        pair.wait()
+    total = summed(mode_slots, doubles)
+    for ref, start in ((dres_ref, 0), (drate_ref, modes)):
+        ref[...] = lax.dot_general(
+            mine_lanes,
+            total[start : start + modes],
+            (((1,), (1,)), ((), ())),
+            precision=HIGHEST,
+            preferred_element_type=F32,
+        )
     for n in range(4):
         settle(landed[n].at[pl.ds(0, PLANE - 1)], in_send.at[n])
     for copy in kept_out:
@@ -575,16 +593,16 @@
     line, reach = steps * SUBS, taps - 1
     vm = pltpu.VMEM
     here = pl.BlockSpec(memory_space=vm)
+    away = pl.BlockSpec(memory_space=pl.ANY)
     dma = pltpu.SemaphoreType.DMA
     tap_rows = -(-3 * taps // SUBS) * SUBS
-    rows = 2 * modes + tap_rows
     ends = modes // WIDE * SUBS
     streams = [x.reshape(view) for x in (queries, key_stream, value_stream, cotangent)]
     results = pl.pallas_call(
         functools.partial(operator_kernel, modes, taps, steps, doubles, scale),
         out_shape=[wide] * 4 + [jax.ShapeDtypeStruct((PLANE, tap_rows, LANES), F32), mode_shape, mode_shape],
-        in_specs=[here] * 7,
-        out_specs=[here] * 7,
+        in_specs=[away] * 4 + [here] * 3,
+        out_specs=[away] * 4 + [here] * 3,
         scratch_shapes=[vm((PLANE, TALL, own, steps), BF16)] * 8
         + [vm((line + reach * SUBS, LANES), F32)] * 4
         + [vm((line, LANES), F32)] * 7
@@ -606,15 +624,18 @@
             vm((TALL, ends, LANES), F32),
             vm((3, reach * SUBS, LANES), F32),
             vm((3, reach * SUBS, LANES), F32),
-            vm((rows, LANES), F32),
-            vm((TALL, rows, LANES), F32),
-            vm((doubles + 1, rows, LANES), F32),
+            vm((tap_rows, LANES), F32),
+            vm((TALL, tap_rows, LANES), F32),
+            vm((doubles + 1, tap_rows, LANES), F32),
+            vm((2 * modes, LANES), F32),
+            vm((TALL, 2 * modes, LANES), F32),
+            vm((doubles + 1, 2 * modes, LANES), F32),
             vm((tap_rows, LANES), F32),
         ]
         + [dma((4,))] * 4
-        + [dma((14,)), dma((doubles,)), dma((doubles,))]
+        + [dma((16,)), dma((2 * doubles,)), dma((2 * doubles,))]
         + [dma((3,))] * 4
-        + [dma((4,))] * 2
+        + [dma((5,))] * 2
         + [dma, dma],
         compiler_params=pltpu.CompilerParams(collective_id=0, has_side_effects=True),
     )(*streams, short_taps, residues, decay_rates)

time: 68.5 us -> 58.5 us (0.85)
  Pallas kernels: 67.8 us -> 57.7 us
    pallas_call x1, Pallas kernels: 65.4 us -> 55.4 us  [per_device(): pl.pallas_call(functools.partial(operator_kernel, modes, taps, steps, dou...]
where the time goes in v5:
time: 58.5 us; the launch traced here: 58.3 us
  Pallas kernels  57.7 us (99%)
  between operations  0.64 us (1%)
    pallas_call x1, Pallas kernels, per_device(): pl.pallas_call(functools.partial(operator_kernel, modes, taps, steps, dou...  55.4 us
    pallas_call x1, Pallas kernels, per_device(): pl.pallas_call(functools.partial(closing_kernel, own, taps), out_shape=[j...  2.31 us

profile of v5, /device:TPU:1, one launch (start us, length us, event | category | flops | bytes accessed | tf_op | source)
XLA Modules:
  0.0 58.3 jit_solution(4979802435464988858)
XLA Ops:
  0.6 55.4 %shard_map.126 = (bf16[2,8,4,16,128]{4,3,2,1,0:T(8,128)(2,1)}, bf16[2,8,4,16,128]{4,3,2,1,0:T(8,128)(2,1)}, bf16[2,8,4,16,128]{4,3,2,1,0:T(8,128)(2,1)}, bf16[2,...) custom-call(bf16[2,8,4,16,128]{4,3,2,1,0:T(8,128)(2,1)} %bitcast.4, ...), custom_call_target="tpu_custom_call" | custom-call | tf_op jit(solution)/shard_map/pallas_call | solution.py:601
  56.0 2.3 %shard_map.127 = (bf16[1,1024,128]{2,1,0:T(8,128)(2,1)}, bf16[1,1024,128]{2,1,0:T(8,128)(2,1)}, bf16[1,1024,128]{2,1,0:T(8,128)(2,1)}, bf16[1,1024,128]{2,1,0:T(...) custom-call(bf16[2,8,4,16,128]{4,3,2,1,0:T(8,128)(2,1)} %get-tuple-element.14.refs_0_, ...), custom_call_target="tpu_custom_call" | custom-call | tf_op jit(solution)/shard_map/pallas_call | solution.py:642

commit v6 on v5

--- a/solution.py
+++ b/solution.py
@@ -13,10 +13,11 @@
 HIGHEST = lax.Precision.HIGHEST
 LANES = 128
 SUBS = 8
-GROUP = 8
+GROUP = 16
 TALL = 8
 WIDE = 4
 PLANE = 8
+PAIR = 2
 
 
 def rounded(x):
@@ -48,7 +49,7 @@
     xq, xk, xv, xc, qs, ks, vs, gs, us, ys, ss, aq, ak, av,
     tab, logs, lst, pst, past, qacc, racc, tacc,
     tsrc, tin, fsrc, fin, bsrc, bin_, rims, tails,
-    tap_part, tap_stack, tap_slots, mode_part, mode_stack, mode_slots, total_ref,
+    tap_part, tap_stack, mode_part, mode_stack, mode_slots, total_ref,
     in_send, in_recv, out_send, out_recv, keep_sem, pair_send, pair_recv,
     rim_send, rim_recv, tail_send, tail_recv, line_send, line_recv, tap_send, tap_recv,
 ):
@@ -65,14 +66,26 @@
     def along(step):
         return {"context": context_of(y, lax.rem(z + step, TALL), x)}
 
-    for step in range(1, PLANE):
-        pl.semaphore_signal(barrier, inc=1, device_id=across(step)[1], device_id_type=MESH)
-    for step in range(1, TALL):
-        pl.semaphore_signal(barrier, inc=1, device_id=along(step), device_id_type=MESH)
-    for step in range(1, doubles):
-        pl.semaphore_signal(
-            barrier, inc=1, device_id={"dp": lax.rem(mine + step, doubles)}, device_id_type=MESH
-        )
+    outer, inner = mine // PAIR, lax.rem(mine, PAIR)
+    tower, field = z * PAIR + inner, spot * PAIR + outer
+
+    def in_tower(step):
+        q = lax.rem(tower + step, TALL * PAIR)
+        return {"dp": outer * PAIR + lax.rem(q, PAIR), "context": context_of(y, q // PAIR, x)}
+
+    def in_field(step):
+        q = lax.rem(field + step, PLANE * PAIR)
+        s = q // PAIR
+        return {
+            "dp": lax.rem(q, PAIR) * PAIR + inner,
+            "context": context_of(s // WIDE, z, lax.rem(s, WIDE)),
+        }
+
+    for step in range(1, TALL * PAIR):
+        pl.semaphore_signal(barrier, inc=1, device_id=in_tower(step), device_id_type=MESH)
+    for step in range(1, PLANE * PAIR):
+        pl.semaphore_signal(barrier, inc=1, device_id=in_field(step), device_id_type=MESH)
+    pl.semaphore_signal(barrier, inc=1, device_id={"dp": doubles - 1 - mine}, device_id_type=MESH)
 
     sources, landed = (k_ref, v_ref, q_ref, c_ref), (mk, mv, mq, mc)
     kept = [
@@ -135,7 +148,7 @@
         copy.wait()
         settle(dst.at[pl.ds(0, TALL - 1)], line_send.at[n], line_recv.at[n])
 
-    pl.semaphore_wait(barrier, PLANE + TALL + doubles - 3)
+    pl.semaphore_wait(barrier, TALL * PAIR + PLANE * PAIR - 1)
     table_copy = line(tsrc, tin, 0)
     for n in range(4):
         for step in range(1, PLANE):
@@ -369,7 +382,7 @@
             return tuple(new_s), tuple(new_f)
 
         few = tuple(zero for _ in members)
-        _, firsts = lax.fori_loop(0, steps, forward, (tuple(lst[fixed(m), :] for m in members), few), unroll=2)
+        _, firsts = lax.fori_loop(0, steps, forward, (tuple(lst[fixed(m), :] for m in members), few), unroll=4)
         for n, m in enumerate(members):
             qacc[pl.ds(m, 1), :] = jnp.sum(firsts[n], axis=0, keepdims=True)
 
@@ -413,7 +426,7 @@
         copy.start()
         kept_out.append(copy)
 
-    sums = lax.fori_loop(0, steps, query_products, tuple(zero for _ in range(taps)), unroll=2)
+    sums = lax.fori_loop(0, steps, query_products, tuple(zero for _ in range(taps)), unroll=4)
     for n in range(taps):
         tacc[pl.ds(n, 1), :] = jnp.sum(sums[n], axis=0, keepdims=True)
     query_tail = tail_copy(0, aq)
@@ -449,7 +462,7 @@
             return tuple(new_s), tuple(new_r)
 
         few = tuple(zero for _ in members)
-        _, seconds = lax.fori_loop(0, steps, backward, (tuple(pst[fixed(m), :] for m in members), few), unroll=2)
+        _, seconds = lax.fori_loop(0, steps, backward, (tuple(pst[fixed(m), :] for m in members), few), unroll=4)
         for n, m in enumerate(members):
             racc[pl.ds(m, 1), :] = jnp.sum(seconds[n], axis=0, keepdims=True)
 
@@ -468,7 +481,7 @@
         ss[at(t), :] = gradient(av, 2, t)
         return carry
 
-    sums = lax.fori_loop(0, steps, pair_products, tuple(zero for _ in range(2 * taps)), unroll=2)
+    sums = lax.fori_loop(0, steps, pair_products, tuple(zero for _ in range(2 * taps)), unroll=4)
     for n in range(2 * taps):
         tacc[pl.ds(taps + n, 1), :] = jnp.sum(sums[n], axis=0, keepdims=True)
     tail_copies = [tail_copy(1, ak), tail_copy(2, av)]
@@ -480,7 +493,17 @@
     mode_part[pl.ds(modes, modes), :] = (
         scale * rate * (residue * (damp * damp / size) * first - weighted * second)
     )
-    tap_copy = line(tap_part, tap_stack, 3)
+    for step in range(1, TALL * PAIR):
+        pltpu.make_async_remote_copy(
+            src_ref=tap_part,
+            dst_ref=tap_stack.at[tower],
+            send_sem=line_send.at[3],
+            recv_sem=line_recv.at[3],
+            device_id=in_tower(step),
+            device_id_type=MESH,
+        ).start()
+    tap_copy = pltpu.make_async_copy(tap_part, tap_stack.at[tower], keep_sem.at[11])
+    tap_copy.start()
     mode_copy = line(mode_part, mode_stack, 4)
     lax.fori_loop(0, steps - reach, pair_gradients, 0, unroll=6)
     for copy in tail_copies:
@@ -500,43 +523,36 @@
             total = total + ref[n]
         return total
 
-    def pairs_of(ref, base):
-        local = pltpu.make_async_copy(ref.at[doubles], ref.at[mine], keep_sem.at[13 + base])
-        copies = [
-            pltpu.make_async_remote_copy(
-                src_ref=ref.at[doubles],
-                dst_ref=ref.at[mine],
-                send_sem=pair_send.at[base * doubles + step],
-                recv_sem=pair_recv.at[base * doubles + step],
-                device_id={"dp": lax.rem(mine + step, doubles)},
-                device_id_type=MESH,
-            )
-            for step in range(1, doubles)
-        ]
-        for copy in copies + [local]:
-            copy.start()
-        return copies + [local]
-
-    line_wait(tap_copy, tap_stack, 3)
-    tap_slots[doubles] = summed(tap_stack, TALL)
-    tap_pairs = pairs_of(tap_slots, 0)
+    tap_copy.wait()
+    settle(tap_stack.at[pl.ds(0, TALL * PAIR - 1)], line_send.at[3], line_recv.at[3])
+    total_ref[...] = summed(tap_stack, TALL * PAIR)
+    for step in range(1, PLANE * PAIR):
+        pltpu.make_async_remote_copy(
+            src_ref=total_ref,
+            dst_ref=shared_ref.at[field],
+            send_sem=tap_send,
+            recv_sem=tap_recv,
+            device_id=in_field(step),
+            device_id_type=MESH,
+        ).start()
+    own_taps = pltpu.make_async_copy(total_ref, shared_ref.at[field], keep_sem.at[15])
+    own_taps.start()
     line_wait(mode_copy, mode_stack, 4)
     mode_slots[doubles] = summed(mode_stack, TALL)
-    for pair in tap_pairs:
-        pair.wait()
-    total_ref[...] = summed(tap_slots, doubles)
-    mode_pairs = pairs_of(mode_slots, 1)
-    for step in range(1, PLANE):
+    mode_pairs = [
         pltpu.make_async_remote_copy(
-            src_ref=total_ref,
-            dst_ref=shared_ref.at[spot],
-            send_sem=tap_send,
-            recv_sem=tap_recv,
-            device_id=across(step)[1],
+            src_ref=mode_slots.at[doubles],
+            dst_ref=mode_slots.at[mine],
+            send_sem=pair_send.at[step],
+            recv_sem=pair_recv.at[step],
+            device_id={"dp": lax.rem(mine + step, doubles)},
             device_id_type=MESH,
-        ).start()
-    own_taps = pltpu.make_async_copy(total_ref, shared_ref.at[spot], keep_sem.at[15])
-    own_taps.start()
+        )
+        for step in range(1, doubles)
+    ]
+    mode_pairs.append(pltpu.make_async_copy(mode_slots.at[doubles], mode_slots.at[mine], keep_sem.at[13]))
+    for pair in mode_pairs:
+        pair.start()
     for pair in mode_pairs:
         pair.wait()
     total = summed(mode_slots, doubles)
@@ -556,7 +572,7 @@
     for n in range(4):
         settle(results[n].at[pl.ds(0, PLANE - 1)], out_send.at[n])
         settle(outputs[n].at[:, pl.ds(0, TALL - 1)], out_recv.at[n])
-    settle(shared_ref.at[pl.ds(0, PLANE - 1)], tap_send, tap_recv)
+    settle(shared_ref.at[pl.ds(0, PLANE * PAIR - 1)], tap_send, tap_recv)
 
 
 def closing_kernel(own, taps, *refs):
@@ -574,7 +590,8 @@
         value = jnp.zeros((rows, LANES), F32)
         for spot in range(groups):
             z, x = pair * (groups // WIDE) + spot // WIDE, spot % WIDE
-            held = shared_ref[y * WIDE + x]
+            first = (y * WIDE + x) * PAIR
+            held = shared_ref[first] + shared_ref[first + 1]
             held = pltpu.roll(held, (spot - z) * own % LANES, 1)
             value = jnp.where(group == spot, held, value)
         for stream in range(3):
@@ -595,12 +612,12 @@
     here = pl.BlockSpec(memory_space=vm)
     away = pl.BlockSpec(memory_space=pl.ANY)
     dma = pltpu.SemaphoreType.DMA
-    tap_rows = -(-3 * taps // SUBS) * SUBS
+    tap_rows = 3 * taps
     ends = modes // WIDE * SUBS
     streams = [x.reshape(view) for x in (queries, key_stream, value_stream, cotangent)]
     results = pl.pallas_call(
         functools.partial(operator_kernel, modes, taps, steps, doubles, scale),
-        out_shape=[wide] * 4 + [jax.ShapeDtypeStruct((PLANE, tap_rows, LANES), F32), mode_shape, mode_shape],
+        out_shape=[wide] * 4 + [jax.ShapeDtypeStruct((PLANE * PAIR, tap_rows, LANES), F32), mode_shape, mode_shape],
         in_specs=[away] * 4 + [here] * 3,
         out_specs=[away] * 4 + [here] * 3,
         scratch_shapes=[vm((PLANE, TALL, own, steps), BF16)] * 8
@@ -625,15 +642,14 @@
             vm((3, reach * SUBS, LANES), F32),
             vm((3, reach * SUBS, LANES), F32),
             vm((tap_rows, LANES), F32),
-            vm((TALL, tap_rows, LANES), F32),
-            vm((doubles + 1, tap_rows, LANES), F32),
+            vm((TALL * PAIR, tap_rows, LANES), F32),
             vm((2 * modes, LANES), F32),
             vm((TALL, 2 * modes, LANES), F32),
             vm((doubles + 1, 2 * modes, LANES), F32),
             vm((tap_rows, LANES), F32),
         ]
         + [dma((4,))] * 4
-        + [dma((16,)), dma((2 * doubles,)), dma((2 * doubles,))]
+        + [dma((16,)), dma((doubles,)), dma((doubles,))]
         + [dma((3,))] * 4
         + [dma((5,))] * 2
         + [dma, dma],

time: 58.5 us -> 54.8 us (0.937)
  Pallas kernels: 57.7 us -> 54 us
    pallas_call x1, Pallas kernels: 55.4 us -> 51.7 us  [per_device(): pl.pallas_call(functools.partial(operator_kernel, modes, taps, steps, dou...]
where the time goes in v6:
time: 54.8 us; the launch traced here: 54.7 us
  Pallas kernels  54 us (99%)
  between operations  0.64 us (1%)
    pallas_call x1, Pallas kernels, per_device(): pl.pallas_call(functools.partial(operator_kernel, modes, taps, steps, dou...  51.7 us
    pallas_call x1, Pallas kernels, per_device(): pl.pallas_call(functools.partial(closing_kernel, own, taps), out_shape=[j...  2.35 us

profile of v6, /device:TPU:1, one launch (start us, length us, event | category | flops | bytes accessed | tf_op | source)
XLA Modules:
  0.0 54.7 jit_solution(1582657336592982114)
XLA Ops:
  0.6 51.7 %shard_map.126 = (bf16[2,8,4,16,128]{4,3,2,1,0:T(8,128)(2,1)}, bf16[2,8,4,16,128]{4,3,2,1,0:T(8,128)(2,1)}, bf16[2,8,4,16,128]{4,3,2,1,0:T(8,128)(2,1)}, bf16[2,...) custom-call(bf16[2,8,4,16,128]{4,3,2,1,0:T(8,128)(2,1)} %bitcast.4, ...), custom_call_target="tpu_custom_call" | custom-call | tf_op jit(solution)/shard_map/pallas_call | solution.py:618
  52.3 2.3 %shard_map.127 = (bf16[1,1024,128]{2,1,0:T(8,128)(2,1)}, bf16[1,1024,128]{2,1,0:T(8,128)(2,1)}, bf16[1,1024,128]{2,1,0:T(8,128)(2,1)}, bf16[1,1024,128]{2,1,0:T(...) custom-call(bf16[2,8,4,16,128]{4,3,2,1,0:T(8,128)(2,1)} %get-tuple-element.14.refs_0_, ...), custom_call_target="tpu_custom_call" | custom-call | tf_op jit(solution)/shard_map/pallas_call | solution.py:658

commit v7 on v6

--- a/solution.py
+++ b/solution.py
@@ -49,7 +49,7 @@
     xq, xk, xv, xc, qs, ks, vs, gs, us, ys, ss, aq, ak, av,
     tab, logs, lst, pst, past, qacc, racc, tacc,
     tsrc, tin, fsrc, fin, bsrc, bin_, rims, tails,
-    tap_part, tap_stack, mode_part, mode_stack, mode_slots, total_ref,
+    tap_part, tap_stack, first_part, first_stack, mode_part, mode_stack, mode_slots, total_ref,
     in_send, in_recv, out_send, out_recv, keep_sem, pair_send, pair_recv,
     rim_send, rim_recv, tail_send, tail_recv, line_send, line_recv, tap_send, tap_recv,
 ):
@@ -426,11 +426,13 @@
         copy.start()
         kept_out.append(copy)
 
+    first_part[...] = scale * size * qacc[...]
     sums = lax.fori_loop(0, steps, query_products, tuple(zero for _ in range(taps)), unroll=4)
     for n in range(taps):
         tacc[pl.ds(n, 1), :] = jnp.sum(sums[n], axis=0, keepdims=True)
     query_tail = tail_copy(0, aq)
     query_tail.start()
+    first_copy = line(first_part, first_stack, 5)
     pack(ys, oo)
     query_tail.wait()
     tail(0, aq)
@@ -476,8 +478,11 @@
                 new.append(carry[n * taps + j] + grad * x_ref[at(t + reach - j), :])
         return tuple(new)
 
-    def pair_gradients(t, carry):
+    def key_gradients(t, carry):
         ys[at(t), :] = gradient(ak, 1, t)
+        return carry
+
+    def value_gradients(t, carry):
         ss[at(t), :] = gradient(av, 2, t)
         return carry
 
@@ -489,10 +494,7 @@
         copy.start()
     tap_part[...] = scale * tacc[...]
     first, second = qacc[...], racc[...] * damp
-    mode_part[pl.ds(0, modes), :] = scale * size * first
-    mode_part[pl.ds(modes, modes), :] = (
-        scale * rate * (residue * (damp * damp / size) * first - weighted * second)
-    )
+    mode_part[...] = scale * rate * (residue * (damp * damp / size) * first - weighted * second)
     for step in range(1, TALL * PAIR):
         pltpu.make_async_remote_copy(
             src_ref=tap_part,
@@ -505,16 +507,18 @@
     tap_copy = pltpu.make_async_copy(tap_part, tap_stack.at[tower], keep_sem.at[11])
     tap_copy.start()
     mode_copy = line(mode_part, mode_stack, 4)
-    lax.fori_loop(0, steps - reach, pair_gradients, 0, unroll=6)
+    lax.fori_loop(0, steps - reach, key_gradients, 0, unroll=6)
     for copy in tail_copies:
         copy.wait()
     tail(1, ak)
     tail(2, av)
     for t in range(steps - reach, steps):
-        pair_gradients(t, 0)
+        key_gradients(t, 0)
     pack(ys, ok)
+    lax.fori_loop(0, steps // 4, value_gradients, 0, unroll=8)
+    deliver(2)
+    lax.fori_loop(steps // 4, steps, value_gradients, 0, unroll=8)
     pack(ss, ov)
-    deliver(2)
     deliver(3)
 
     def summed(ref, count):
@@ -523,6 +527,8 @@
             total = total + ref[n]
         return total
 
+    line_wait(first_copy, first_stack, 5)
+    mode_slots[doubles, pl.ds(0, modes), :] = summed(first_stack, TALL)
     tap_copy.wait()
     settle(tap_stack.at[pl.ds(0, TALL * PAIR - 1)], line_send.at[3], line_recv.at[3])
     total_ref[...] = summed(tap_stack, TALL * PAIR)
@@ -538,7 +544,7 @@
     own_taps = pltpu.make_async_copy(total_ref, shared_ref.at[field], keep_sem.at[15])
     own_taps.start()
     line_wait(mode_copy, mode_stack, 4)
-    mode_slots[doubles] = summed(mode_stack, TALL)
+    mode_slots[doubles, pl.ds(modes, modes), :] = summed(mode_stack, TALL)
     mode_pairs = [
         pltpu.make_async_remote_copy(
             src_ref=mode_slots.at[doubles],
@@ -550,7 +556,7 @@
         )
         for step in range(1, doubles)
     ]
-    mode_pairs.append(pltpu.make_async_copy(mode_slots.at[doubles], mode_slots.at[mine], keep_sem.at[13]))
+    mode_pairs.append(pltpu.make_async_copy(mode_slots.at[doubles], mode_slots.at[mine], keep_sem.at[14]))
     for pair in mode_pairs:
         pair.start()
     for pair in mode_pairs:
@@ -617,9 +623,9 @@
     streams = [x.reshape(view) for x in (queries, key_stream, value_stream, cotangent)]
     results = pl.pallas_call(
         functools.partial(operator_kernel, modes, taps, steps, doubles, scale),
-        out_shape=[wide] * 4 + [jax.ShapeDtypeStruct((PLANE * PAIR, tap_rows, LANES), F32), mode_shape, mode_shape],
+        out_shape=[vm(view, BF16)] * 4 + [vm((PLANE * PAIR, tap_rows, LANES), F32), vm(residues.shape, F32), vm(residues.shape, F32)],
         in_specs=[away] * 4 + [here] * 3,
-        out_specs=[away] * 4 + [here] * 3,
+        out_specs=[here] * 7,
         scratch_shapes=[vm((PLANE, TALL, own, steps), BF16)] * 8
         + [vm((line + reach * SUBS, LANES), F32)] * 4
         + [vm((line, LANES), F32)] * 7
@@ -643,17 +649,19 @@
             vm((3, reach * SUBS, LANES), F32),
             vm((tap_rows, LANES), F32),
             vm((TALL * PAIR, tap_rows, LANES), F32),
-            vm((2 * modes, LANES), F32),
-            vm((TALL, 2 * modes, LANES), F32),
+            vm((modes, LANES), F32),
+            vm((TALL, modes, LANES), F32),
+            vm((modes, LANES), F32),
+            vm((TALL, modes, LANES), F32),
             vm((doubles + 1, 2 * modes, LANES), F32),
             vm((tap_rows, LANES), F32),
         ]
         + [dma((4,))] * 4
         + [dma((16,)), dma((doubles,)), dma((doubles,))]
         + [dma((3,))] * 4
-        + [dma((5,))] * 2
+        + [dma((6,))] * 2
         + [dma, dma],
-        compiler_params=pltpu.CompilerParams(collective_id=0, has_side_effects=True),
+        compiler_params=pltpu.CompilerParams(collective_id=0, has_side_effects=True, vmem_limit_bytes=58 * 1024 * 1024),
     )(*streams, short_taps, residues, decay_rates)
     return pl.pallas_call(
         functools.partial(closing_kernel, own, taps),
@@ -661,6 +669,7 @@
         + [jax.ShapeDtypeStruct(short_taps.shape, F32), mode_shape, mode_shape],
         in_specs=[here] * 7,
         out_specs=[here] * 7,
+        compiler_params=pltpu.CompilerParams(vmem_limit_bytes=16 * 1024 * 1024),
     )(*results)
 
 

time: 54.8 us -> 52.5 us (0.958)
  Pallas kernels: 54 us -> 51.7 us
    pallas_call x1, Pallas kernels: 2.35 us -> 1.11 us  [per_device(): pl.pallas_call(functools.partial(closing_kernel, own, taps), out_shape=[j...]
    pallas_call x1, Pallas kernels: 51.7 us -> 50.6 us  [per_device(): pl.pallas_call(functools.partial(operator_kernel, modes, taps, steps, dou...]
where the time goes in v7:
time: 52.5 us; the launch traced here: 52.4 us
  Pallas kernels  51.7 us (98%)
  between operations  0.64 us (1%)
    pallas_call x1, Pallas kernels, per_device(): pl.pallas_call(functools.partial(operator_kernel, modes, taps, steps, dou...  50.6 us
    pallas_call x1, Pallas kernels, per_device(): pl.pallas_call(functools.partial(closing_kernel, own, taps), out_shape=[j...  1.11 us

profile of v7, /device:TPU:1, one launch (start us, length us, event | category | flops | bytes accessed | tf_op | source)
XLA Modules:
  0.0 52.4 jit_solution(16804885248414092406)
XLA Ops:
  0.6 50.6 %shard_map.126 = (bf16[2,8,4,16,128]{4,3,2,1,0:T(8,128)(2,1)S(1)}, bf16[2,8,4,16,128]{4,3,2,1,0:T(8,128)(2,1)S(1)}, bf16[2,8,4,16,128]{4,3,2,1,0:T(8,128)(2,1)S(...) custom-call(bf16[2,8,4,16,128]{4,3,2,1,0:T(8,128)(2,1)} %bitcast.4, ...), custom_call_target="tpu_custom_call" | custom-call | tf_op jit(solution)/shard_map/pallas_call | solution.py:624
  51.3 1.1 %shard_map.127 = (bf16[1,1024,128]{2,1,0:T(8,128)(2,1)}, bf16[1,1024,128]{2,1,0:T(8,128)(2,1)}, bf16[1,1024,128]{2,1,0:T(8,128)(2,1)}, bf16[1,1024,128]{2,1,0:T(...) custom-call(bf16[2,8,4,16,128]{4,3,2,1,0:T(8,128)(2,1)S(1)} %get-tuple-element.14.refs_0_, ...), custom_call_target="tpu_custom_call" | custom-call | tf_op jit(solution)/shard_map/pallas_call | solution.py:666

commit v8 on v7

--- a/solution.py
+++ b/solution.py
@@ -508,6 +508,7 @@
     tap_copy.start()
     mode_copy = line(mode_part, mode_stack, 4)
     lax.fori_loop(0, steps - reach, key_gradients, 0, unroll=6)
+    lax.fori_loop(0, steps - reach, value_gradients, 0, unroll=6)
     for copy in tail_copies:
         copy.wait()
     tail(1, ak)
@@ -515,9 +516,9 @@
     for t in range(steps - reach, steps):
         key_gradients(t, 0)
     pack(ys, ok)
-    lax.fori_loop(0, steps // 4, value_gradients, 0, unroll=8)
+    for t in range(steps - reach, steps):
+        value_gradients(t, 0)
     deliver(2)
-    lax.fori_loop(steps // 4, steps, value_gradients, 0, unroll=8)
     pack(ss, ov)
     deliver(3)
 

time: 52.5 us -> 52.5 us (level)
  no operation moved by 1% of the time
where the time goes in v8:
time: 52.5 us; the launch traced here: 52.4 us
  Pallas kernels  51.7 us (98%)
  between operations  0.64 us (1%)
    pallas_call x1, Pallas kernels, per_device(): pl.pallas_call(functools.partial(operator_kernel, modes, taps, steps, dou...  50.6 us
    pallas_call x1, Pallas kernels, per_device(): pl.pallas_call(functools.partial(closing_kernel, own, taps), out_shape=[j...  1.11 us

profile of v8, /device:TPU:1, one launch (start us, length us, event | category | flops | bytes accessed | tf_op | source)
XLA Modules:
  0.0 52.4 jit_solution(13703659794926454064)
XLA Ops:
  0.6 50.6 %shard_map.126 = (bf16[2,8,4,16,128]{4,3,2,1,0:T(8,128)(2,1)S(1)}, bf16[2,8,4,16,128]{4,3,2,1,0:T(8,128)(2,1)S(1)}, bf16[2,8,4,16,128]{4,3,2,1,0:T(8,128)(2,1)S(...) custom-call(bf16[2,8,4,16,128]{4,3,2,1,0:T(8,128)(2,1)} %bitcast.4, ...), custom_call_target="tpu_custom_call" | custom-call | tf_op jit(solution)/shard_map/pallas_call | solution.py:625
  51.3 1.1 %shard_map.127 = (bf16[1,1024,128]{2,1,0:T(8,128)(2,1)}, bf16[1,1024,128]{2,1,0:T(8,128)(2,1)}, bf16[1,1024,128]{2,1,0:T(8,128)(2,1)}, bf16[1,1024,128]{2,1,0:T(...) custom-call(bf16[2,8,4,16,128]{4,3,2,1,0:T(8,128)(2,1)S(1)} %get-tuple-element.14.refs_0_, ...), custom_call_target="tpu_custom_call" | custom-call | tf_op jit(solution)/shard_map/pallas_call | solution.py:667
